TPU v7x, 32 devices: a whole 2x2x4 slice. The times are simulated.
32 devices in a mesh: dp: 4 (over z), context: 4 (over y, core), tensor: 2 (over x).
Axes of the slice: x: 2, y: 2, z: 4, core: 2. Of those that a mesh axis runs over, the one named last changes fastest.
Arguments:
- hidden_in: bfloat16 [16, 2048, 768], P('dp', 'context'), may hold values from -6 to 6
- out_grad: bfloat16 [16, 2048, 768], P('dp', 'context'), may hold values from -6 to 6
- segment_ids: int32 [16, 2048], P('dp'), may hold values from 0 to 15, never falling along the last dimension, each value on 1 to 1024 neighbouring positions
- token_valid: int32 [16, 2048], P('dp'), may hold values 0 or 1
- random_blocks: int32 [16, 32, 3], P('dp'), may hold values from 2 to 31, as said below
- query_weight: bfloat16 [768, 768], P('dp', 'tensor'), may hold values from -0.21875 to 0.21875
- query_bias: bfloat16 [768], P('tensor'), may hold values from -3 to 3
- key_weight: bfloat16 [768, 768], P('dp', 'tensor'), may hold values from -0.21875 to 0.21875
- value_weight: bfloat16 [768, 768], P('dp', 'tensor'), may hold values from -0.21875 to 0.21875
- value_bias: bfloat16 [768], P('tensor'), may hold values from -3 to 3
- output_weight: bfloat16 [768, 768], P('tensor', 'dp'), may hold values from -0.625 to 0.625
- output_bias: bfloat16 [768], replicated, may hold values from -3 to 3
- norm1_gain: bfloat16 [768], replicated, may hold values from 0.5 to 1.5
- norm1_shift: bfloat16 [768], replicated, may hold values from -3 to 3
- up_weight: bfloat16 [768, 3072], P('dp', 'tensor'), may hold values from -0.21875 to 0.21875
- up_bias: bfloat16 [3072], P('tensor'), may hold values from -3 to 3
- down_weight: bfloat16 [3072, 768], P('tensor', 'dp'), may hold values from -0.109375 to 0.109375
- down_bias: bfloat16 [768], replicated, may hold values from -3 to 3
- norm2_gain: bfloat16 [768], replicated, may hold values from 0.5 to 1.5
- norm2_shift: bfloat16 [768], replicated, may hold values from -3 to 3
Outputs:
- layer_out: bfloat16 [16, 2048, 768], P('dp', 'context')
- input_grad: float32 [16, 2048, 768], P('dp', 'context')
- query_weight_grad: float32 [768, 768], P('dp', 'tensor')
- query_bias_grad: float32 [768], P('tensor')
- key_weight_grad: float32 [768, 768], P('dp', 'tensor')
- value_weight_grad: float32 [768, 768], P('dp', 'tensor')
- value_bias_grad: float32 [768], P('tensor')
- output_weight_grad: float32 [768, 768], P('tensor', 'dp')
- output_bias_grad: float32 [768], replicated
- norm1_gain_grad: float32 [768], replicated
- norm1_shift_grad: float32 [768], replicated
- up_weight_grad: float32 [768, 3072], P('dp', 'tensor')
- up_bias_grad: float32 [3072], P('tensor')
- down_weight_grad: float32 [3072, 768], P('tensor', 'dp')
- down_bias_grad: float32 [768], replicated
- norm2_gain_grad: float32 [768], replicated
- norm2_shift_grad: float32 [768], replicated
- input_rms: float32 [5], replicated
Inputs may be any that keep to these rules, and one draw needn't show every extreme that they name: `random_blocks`: for query block b the 3 numbers are distinct, none is 0, 1, b - 1, b or b + 1. `segment_ids`: numbers never fall along a sequence; a document spans 1 to 1024 tokens.
All inputs are finite; a program needn't handle non-finite values. No bound on the sum of `token_valid` on one device may be relied on, other than what follows from the above.
Results may differ from a plain program's by a relative error of at most 0.019.
Values may be sent and summed in bfloat16 or wider, within the bound.
A program may use at most 384 MiB of HBM per device.

v0:
```python
import jax
import jax.numpy as jnp
from jax import lax
from jax.sharding import PartitionSpec as P

HD = 64
BLK = 64


EPSILON = 1e-06
NEG_FILL = -1e30


def layer_norm(values, norm_gain, norm_shift):
    row_mean = jnp.mean(values, -1, keepdims=True)
    centered = values - row_mean
    row_var = jnp.mean(centered * centered, -1, keepdims=True)
    return centered * lax.rsqrt(row_var + EPSILON) * norm_gain + norm_shift


def gelu_tanh(values):
    return jax.nn.gelu(values, approximate=True)


def slot_table(first_block, local_blocks, all_blocks, random_local):
    block_ids = first_block + jnp.arange(local_blocks, dtype=jnp.int32)
    near_ids = jnp.stack([block_ids - 1, block_ids, block_ids + 1], -1)
    global_ids = jnp.broadcast_to(jnp.arange(2, dtype=jnp.int32), (local_blocks, 2))
    fixed_ids = jnp.concatenate([near_ids, global_ids], -1)
    near_ok = jnp.stack(
        [block_ids >= 3, block_ids >= 2, (block_ids >= 1) & (block_ids <= all_blocks - 2)], -1
    )
    fixed_ok = jnp.concatenate([near_ok, jnp.ones((local_blocks, 2), jnp.bool_)], -1)
    seq_count = random_local.shape[0]
    slot_ids = jnp.concatenate(
        [jnp.broadcast_to(fixed_ids, (seq_count,) + fixed_ids.shape), random_local], -1
    )
    slot_ok = jnp.concatenate(
        [
            jnp.broadcast_to(fixed_ok, (seq_count,) + fixed_ok.shape),
            jnp.ones(random_local.shape, jnp.bool_),
        ],
        -1,
    )
    return (jnp.clip(slot_ids, 0, all_blocks - 1), slot_ok)


def pick_rows(table, index_set):
    return jax.vmap(lambda one_table, one_index: one_table[one_index])(table, index_set)


def pick_tiles(table, index_set):
    seq_count, heads_local, all_blocks, block_len, head_size = table.shape
    local_blocks, slot_count = (index_set.shape[1], index_set.shape[2])
    picked = jax.vmap(lambda one_table, one_index: one_table[:, one_index])(table, index_set)
    return picked.reshape(seq_count, heads_local, local_blocks, slot_count * block_len, head_size)


def to_heads(rows, heads_local):
    seq_count, length, part_width = rows.shape
    return rows.reshape(seq_count, length, heads_local, part_width // heads_local).transpose(
        0, 2, 1, 3
    )


def from_heads(split):
    seq_count, heads_local, length, head_size = split.shape
    return split.transpose(0, 2, 1, 3).reshape(seq_count, length, heads_local * head_size)


def sparse_mask(slot_ids, slot_ok, first_block, block_len, segments, valid_keys):
    seq_count, local_blocks, slot_count = slot_ids.shape
    offsets = jnp.arange(block_len, dtype=jnp.int32)
    key_pos = (slot_ids[..., None] * block_len + offsets).reshape(
        seq_count, local_blocks, slot_count * block_len
    )
    query_pos = (first_block + jnp.arange(local_blocks, dtype=jnp.int32))[
        :, None
    ] * block_len + offsets
    key_seg = pick_rows(segments, key_pos)
    key_live = pick_rows(valid_keys, key_pos)
    query_seg = pick_rows(segments, jnp.broadcast_to(query_pos, (seq_count,) + query_pos.shape))
    slot_live = jnp.repeat(slot_ok, block_len, axis=-1)
    same_doc = (query_seg[..., :, None] == key_seg[..., None, :]) & (key_live[..., None, :] == 1)
    self_pair = query_pos[None, :, :, None] == key_pos[:, :, None, :]
    return slot_live[:, :, None, :] & (same_doc | self_pair)


def dense_mask(glob_len, segments, valid_keys):
    full_len = segments.shape[1]
    same_doc = (segments[:, :glob_len, None] == segments[:, None, :]) & (
        valid_keys[:, None, :] == 1
    )
    self_pair = jnp.arange(glob_len)[:, None] == jnp.arange(full_len)[None, :]
    return same_doc | self_pair[None]


def softmax_rows(masked):
    row_top = jnp.max(masked, -1, keepdims=True)
    shifted_exp = jnp.exp(masked - row_top)
    totals = jnp.sum(shifted_exp, -1, keepdims=True)
    return (shifted_exp / totals, row_top + jnp.log(totals))


def place_tiles(grad_sel, ids_flat, all_blocks, block_len):
    seq_count, heads_local = (grad_sel.shape[0], grad_sel.shape[1])
    head_size = grad_sel.shape[-1]
    slot_total = ids_flat.shape[1]
    pieces = grad_sel.reshape(seq_count, heads_local, slot_total, block_len, head_size)
    zero_grid = jnp.zeros((seq_count, heads_local, all_blocks, block_len, head_size), jnp.float32)
    summed_in = jax.vmap(lambda acc_one, ids_one, vals_one: acc_one.at[:, ids_one].add(vals_one))(
        zero_grid, ids_flat, pieces
    )
    return from_heads(summed_in.reshape(seq_count, heads_local, all_blocks * block_len, head_size))


def local(
    hidden_in,
    out_grad,
    segment_ids,
    token_valid,
    random_blocks,
    query_weight,
    query_bias,
    key_weight,
    value_weight,
    value_bias,
    output_weight,
    output_bias,
    norm1_gain,
    norm1_shift,
    up_weight,
    up_bias,
    down_weight,
    down_bias,
    norm2_gain,
    norm2_shift,
):
    seq_count, local_len, width = hidden_in.shape
    full_len = segment_ids.shape[1]
    block_len = BLK
    local_blocks = local_len // block_len
    all_blocks = full_len // block_len
    glob_len = 2 * block_len
    row_count = seq_count * local_len
    score_scale = HD ** (-0.5)
    place_index = lax.axis_index("context")
    at_front = place_index == 0
    w_query, w_key, w_value, w_out = (
        lax.all_gather(query_weight, "dp", axis=0, tiled=True),
        lax.all_gather(key_weight, "dp", axis=0, tiled=True),
        lax.all_gather(value_weight, "dp", axis=0, tiled=True),
        lax.all_gather(output_weight, "dp", axis=1, tiled=True),
    )
    w_up, w_down = (
        lax.all_gather(up_weight, "dp", axis=0, tiled=True),
        lax.all_gather(down_weight, "dp", axis=1, tiled=True),
    )
    part_width = w_query.shape[1]
    heads_local = part_width // HD
    x_low = hidden_in.reshape(row_count, width)
    x_full = x_low.astype(jnp.float32)
    q_rows = (
        jnp.dot(x_low, w_query, preferred_element_type=jnp.float32) + query_bias.astype(jnp.float32)
    ).astype(jnp.bfloat16)
    k_rows = jnp.dot(x_low, w_key, preferred_element_type=jnp.float32).astype(jnp.bfloat16)
    v_rows = (
        jnp.dot(x_low, w_value, preferred_element_type=jnp.float32) + value_bias.astype(jnp.float32)
    ).astype(jnp.bfloat16)
    k_full, v_full = (
        lax.all_gather(
            k_rows.reshape(seq_count, local_len, part_width), "context", axis=1, tiled=True
        ),
        lax.all_gather(
            v_rows.reshape(seq_count, local_len, part_width), "context", axis=1, tiled=True
        ),
    )
    k_heads = to_heads(k_full, heads_local)
    v_heads = to_heads(v_full, heads_local)
    q_heads = to_heads(q_rows.reshape(seq_count, local_len, part_width), heads_local)
    tile_shape = (seq_count, heads_local, all_blocks, block_len, HD)
    first_block = place_index * local_blocks
    random_local = lax.dynamic_slice_in_dim(random_blocks, first_block, local_blocks, 1)
    slot_ids, slot_ok = slot_table(first_block, local_blocks, all_blocks, random_local)
    allowed = sparse_mask(slot_ids, slot_ok, first_block, block_len, segment_ids, token_valid)[
        :, None
    ]
    slot_count = slot_ids.shape[2]
    key_sel = pick_tiles(k_heads.reshape(tile_shape), slot_ids)
    value_sel = pick_tiles(v_heads.reshape(tile_shape), slot_ids)
    query_blocks = q_heads.reshape(seq_count, heads_local, local_blocks, block_len, HD)

    def sparse_scores():
        raw_scores = (
            jnp.einsum(
                "shnqd,shnkd->shnqk", query_blocks, key_sel, preferred_element_type=jnp.float32
            )
            * score_scale
        )
        return jnp.where(allowed, raw_scores, NEG_FILL)

    fwd_probs, lse_sparse = softmax_rows(sparse_scores())
    o_split = jnp.einsum(
        "shnqk,shnkd->shnqd",
        fwd_probs.astype(jnp.bfloat16),
        value_sel,
        preferred_element_type=jnp.float32,
    ).astype(jnp.bfloat16)
    o_sparse = from_heads(o_split.reshape(seq_count, heads_local, local_len, HD))
    query_glob = q_heads[:, :, :glob_len]
    glob_allowed = dense_mask(glob_len, segment_ids, token_valid)[:, None]

    def dense_scores():
        raw_scores = (
            jnp.einsum("shqd,shkd->shqk", query_glob, k_heads, preferred_element_type=jnp.float32)
            * score_scale
        )
        return jnp.where(glob_allowed, raw_scores, NEG_FILL)

    def dense_on(operand):
        glob_probs, glob_lse = softmax_rows(dense_scores())
        glob_out = jnp.einsum(
            "shqk,shkd->shqd",
            glob_probs.astype(jnp.bfloat16),
            v_heads,
            preferred_element_type=jnp.float32,
        ).astype(jnp.bfloat16)
        return (from_heads(glob_out), glob_lse)

    def dense_off(operand):
        return (
            jnp.zeros((seq_count, glob_len, part_width), jnp.bfloat16),
            jnp.zeros((seq_count, heads_local, glob_len, 1), jnp.float32),
        )

    o_glob, lse_glob = lax.cond(at_front, dense_on, dense_off, 0)
    o_front = jnp.where(at_front, o_glob, o_sparse[:, :glob_len])
    attended = jnp.concatenate([o_front, o_sparse[:, glob_len:]], 1).reshape(row_count, part_width)
    attn_part = jnp.dot(attended, w_out, preferred_element_type=jnp.float32)
    attn_out = lax.psum(attn_part, "tensor") + output_bias.astype(jnp.float32)
    first_sum = x_full + attn_out
    gain_one = norm1_gain.astype(jnp.float32)
    shift_one = norm1_shift.astype(jnp.float32)
    normed = layer_norm(first_sum, gain_one, shift_one)
    normed_low = normed.astype(jnp.bfloat16)
    pre_act = jnp.dot(normed_low, w_up, preferred_element_type=jnp.float32) + up_bias.astype(
        jnp.float32
    )
    act_low = gelu_tanh(pre_act).astype(jnp.bfloat16)
    ffn_part = jnp.dot(act_low, w_down, preferred_element_type=jnp.float32)
    ffn_out = lax.psum(ffn_part, "tensor") + down_bias.astype(jnp.float32)
    second_sum = normed + ffn_out
    gain_two = norm2_gain.astype(jnp.float32)
    shift_two = norm2_shift.astype(jnp.float32)
    layer_out, norm_back = jax.vjp(layer_norm, second_sum, gain_two, shift_two)
    g_second, gain_two_grad, shift_two_grad = norm_back(
        out_grad.reshape(row_count, width).astype(jnp.float32)
    )
    g_ffn = g_second.astype(jnp.bfloat16)
    down_bias_grad = jnp.sum(g_ffn.astype(jnp.float32), 0)
    down_part = jnp.dot(act_low.T, g_ffn, preferred_element_type=jnp.float32)
    g_act = jnp.dot(g_ffn, w_down.T, preferred_element_type=jnp.float32)
    g_pre = jax.vjp(gelu_tanh, pre_act)[1](g_act)[0].astype(jnp.bfloat16)
    up_bias_grad = jnp.sum(g_pre.astype(jnp.float32), 0)
    up_part = jnp.dot(normed_low.T, g_pre, preferred_element_type=jnp.float32)
    g_normed = g_second + lax.psum(
        jnp.dot(g_pre, w_up.T, preferred_element_type=jnp.float32), "tensor"
    )
    g_first, gain_one_grad, shift_one_grad = jax.vjp(layer_norm, first_sum, gain_one, shift_one)[1](
        g_normed
    )
    g_attn = g_first.astype(jnp.bfloat16)
    out_bias_grad = jnp.sum(g_attn.astype(jnp.float32), 0)
    out_part = jnp.dot(attended.T, g_attn, preferred_element_type=jnp.float32)
    g_attended = (
        jnp.dot(g_attn, w_out.T, preferred_element_type=jnp.float32)
        .astype(jnp.bfloat16)
        .reshape(seq_count, local_len, part_width)
    )
    front_rows = (jnp.arange(local_len) < glob_len) & at_front
    g_masked = jnp.where(front_rows[None, :, None], jnp.zeros_like(g_attended), g_attended)
    g_sparse = to_heads(g_masked, heads_local).reshape(
        seq_count, heads_local, local_blocks, block_len, HD
    )
    sparse_probs = jnp.exp(sparse_scores() - lse_sparse)
    g_probs = jnp.einsum(
        "shnqd,shnkd->shnqk", g_sparse, value_sel, preferred_element_type=jnp.float32
    )
    g_scores = (
        sparse_probs * (g_probs - jnp.sum(sparse_probs * g_probs, -1, keepdims=True))
    ).astype(jnp.bfloat16)
    g_query_split = (
        jnp.einsum("shnqk,shnkd->shnqd", g_scores, key_sel, preferred_element_type=jnp.float32)
        * score_scale
    )
    g_glob = to_heads(g_attended[:, :glob_len], heads_local)

    def dense_back(operand):
        glob_probs = jnp.exp(dense_scores() - lse_glob)
        g_probs_glob = jnp.einsum(
            "shqd,shkd->shqk", g_glob, v_heads, preferred_element_type=jnp.float32
        )
        g_value_glob = jnp.einsum(
            "shqk,shqd->shkd",
            glob_probs.astype(jnp.bfloat16),
            g_glob,
            preferred_element_type=jnp.float32,
        )
        g_scores_glob = (
            glob_probs * (g_probs_glob - jnp.sum(glob_probs * g_probs_glob, -1, keepdims=True))
        ).astype(jnp.bfloat16)
        g_query_glob = (
            jnp.einsum(
                "shqk,shkd->shqd", g_scores_glob, k_heads, preferred_element_type=jnp.float32
            )
            * score_scale
        )
        g_key_glob = (
            jnp.einsum(
                "shqk,shqd->shkd", g_scores_glob, query_glob, preferred_element_type=jnp.float32
            )
            * score_scale
        )
        return (from_heads(g_query_glob), from_heads(g_key_glob), from_heads(g_value_glob))

    def dense_none(operand):
        return (
            jnp.zeros((seq_count, glob_len, part_width), jnp.float32),
            jnp.zeros((seq_count, full_len, part_width), jnp.float32),
            jnp.zeros((seq_count, full_len, part_width), jnp.float32),
        )

    gq_glob, gk_glob, gv_glob = lax.cond(at_front, dense_back, dense_none, 0)
    g_value_sel = jnp.einsum(
        "shnqk,shnqd->shnkd",
        sparse_probs.astype(jnp.bfloat16),
        g_sparse,
        preferred_element_type=jnp.float32,
    )
    g_key_sel = (
        jnp.einsum("shnqk,shnqd->shnkd", g_scores, query_blocks, preferred_element_type=jnp.float32)
        * score_scale
    )
    ids_local = slot_ids.reshape(seq_count, local_blocks * slot_count)
    g_key_all = place_tiles(g_key_sel, ids_local, all_blocks, block_len) + gk_glob
    g_value_all = place_tiles(g_value_sel, ids_local, all_blocks, block_len) + gv_glob
    g_key_mine, g_value_mine = (
        lax.psum_scatter(
            g_key_all.astype(jnp.bfloat16), "context", scatter_dimension=1, tiled=True
        ).astype(jnp.float32),
        lax.psum_scatter(
            g_value_all.astype(jnp.bfloat16), "context", scatter_dimension=1, tiled=True
        ).astype(jnp.float32),
    )
    g_query_sp = from_heads(g_query_split.reshape(seq_count, heads_local, local_len, HD))
    query_front = jnp.where(at_front, gq_glob, g_query_sp[:, :glob_len])
    g_query = (
        jnp.concatenate([query_front, g_query_sp[:, glob_len:]], 1)
        .reshape(row_count, part_width)
        .astype(jnp.bfloat16)
    )
    g_key = g_key_mine.reshape(row_count, part_width).astype(jnp.bfloat16)
    g_value = g_value_mine.reshape(row_count, part_width).astype(jnp.bfloat16)
    query_bias_grad = jnp.sum(g_query.astype(jnp.float32), 0)
    value_bias_grad = jnp.sum(g_value.astype(jnp.float32), 0)
    query_part = jnp.dot(x_low.T, g_query, preferred_element_type=jnp.float32)
    key_part = jnp.dot(x_low.T, g_key, preferred_element_type=jnp.float32)
    value_part = jnp.dot(x_low.T, g_value, preferred_element_type=jnp.float32)
    back_part = jnp.dot(g_query, w_query.T, preferred_element_type=jnp.float32)
    back_part = back_part + jnp.dot(g_key, w_key.T, preferred_element_type=jnp.float32)
    back_part = back_part + jnp.dot(g_value, w_value.T, preferred_element_type=jnp.float32)
    input_grad = g_first + lax.psum(back_part.astype(jnp.bfloat16), "tensor").astype(jnp.float32)
    valid_rows = (
        lax.dynamic_slice_in_dim(token_valid, place_index * local_len, local_len, 1)
        .reshape(row_count)
        .astype(jnp.float32)
    )

    def squares(member):
        return jnp.sum(valid_rows * jnp.sum(member * member, -1))

    stat_terms = jnp.stack(
        [
            squares(x_full),
            squares(first_sum),
            squares(second_sum),
            squares(attn_out),
            squares(ffn_out),
            jnp.sum(valid_rows),
        ]
    )
    (
        bias_q_sum,
        bias_v_sum,
        bias_o_sum,
        gain_one_sum,
        shift_one_sum,
        bias_up_sum,
        bias_down_sum,
        gain_two_sum,
        shift_two_sum,
        stat_sums,
    ) = lax.psum(
        (
            query_bias_grad,
            value_bias_grad,
            out_bias_grad,
            gain_one_grad,
            shift_one_grad,
            up_bias_grad,
            down_bias_grad,
            gain_two_grad,
            shift_two_grad,
            stat_terms,
        ),
        ("dp", "context"),
    )
    input_rms = jnp.sqrt(stat_sums[:5] / (jnp.maximum(stat_sums[5], 1.0) * width))
    piece_q, piece_k, piece_v, piece_o, piece_up, piece_down = (
        lax.psum_scatter(
            query_part.astype(jnp.bfloat16), "dp", scatter_dimension=0, tiled=True
        ).astype(jnp.float32),
        lax.psum_scatter(
            key_part.astype(jnp.bfloat16), "dp", scatter_dimension=0, tiled=True
        ).astype(jnp.float32),
        lax.psum_scatter(
            value_part.astype(jnp.bfloat16), "dp", scatter_dimension=0, tiled=True
        ).astype(jnp.float32),
        lax.psum_scatter(
            out_part.astype(jnp.bfloat16), "dp", scatter_dimension=1, tiled=True
        ).astype(jnp.float32),
        lax.psum_scatter(
            up_part.astype(jnp.bfloat16), "dp", scatter_dimension=0, tiled=True
        ).astype(jnp.float32),
        lax.psum_scatter(
            down_part.astype(jnp.bfloat16), "dp", scatter_dimension=1, tiled=True
        ).astype(jnp.float32),
    )
    shard_q, shard_k, shard_v, shard_o, shard_up, shard_down = (
        lax.psum(piece_q.astype(jnp.bfloat16), "context").astype(jnp.float32),
        lax.psum(piece_k.astype(jnp.bfloat16), "context").astype(jnp.float32),
        lax.psum(piece_v.astype(jnp.bfloat16), "context").astype(jnp.float32),
        lax.psum(piece_o.astype(jnp.bfloat16), "context").astype(jnp.float32),
        lax.psum(piece_up.astype(jnp.bfloat16), "context").astype(jnp.float32),
        lax.psum(piece_down.astype(jnp.bfloat16), "context").astype(jnp.float32),
    )
    return (
        layer_out.astype(jnp.bfloat16).reshape(seq_count, local_len, width),
        input_grad.reshape(seq_count, local_len, width),
        shard_q,
        bias_q_sum,
        shard_k,
        shard_v,
        bias_v_sum,
        shard_o,
        bias_o_sum,
        gain_one_sum,
        shift_one_sum,
        shard_up,
        bias_up_sum,
        shard_down,
        bias_down_sum,
        gain_two_sum,
        shift_two_sum,
        input_rms,
    )


def solution(mesh):
    return jax.shard_map(
        local,
        mesh=mesh,
        in_specs=(
            P("dp", "context", None),
            P("dp", "context", None),
            P("dp", None),
            P("dp", None),
            P("dp", None, None),
            P("dp", "tensor"),
            P("tensor"),
            P("dp", "tensor"),
            P("dp", "tensor"),
            P("tensor"),
            P("tensor", "dp"),
            P(),
            P(),
            P(),
            P("dp", "tensor"),
            P("tensor"),
            P("tensor", "dp"),
            P(),
            P(),
            P(),
        ),
        out_specs=(
            P("dp", "context", None),
            P("dp", "context", None),
            P("dp", "tensor"),
            P("tensor"),
            P("dp", "tensor"),
            P("dp", "tensor"),
            P("tensor"),
            P("tensor", "dp"),
            P(),
            P(),
            P(),
            P("dp", "tensor"),
            P("tensor"),
            P("tensor", "dp"),
            P(),
            P(),
            P(),
            P(),
        ),
        check_vma=False,
    )
```

profile of v0, /device:TPU:0, one launch (start us, length us, event | category | flops | bytes accessed | tf_op | source)
XLA Modules:
  0.0 2411.7 jit_solution(1469488979690730911)
XLA Ops:
  99.5 138.1 %gather_fusion.1 = s32[16384]{0:T(1024)S(1)} fusion(s32[4,2048]{1,0:T(4,128)S(1)} %copy-done.2, s32[16384]{0:T(1024)S(1)} %bitcast.218), kind=kCustom, calls=%fused_computation.1 | custom fusion | bytes 262144 | tf_op jit(solution)/shard_map/vmap()/gather | solution.py:49
  237.6 138.1 %gather_fusion.2 = s32[16384]{0:T(1024)S(1)} fusion(s32[4,2048]{1,0:T(4,128)S(1)} %copy-done.3, s32[16384]{0:T(1024)S(1)} %bitcast.219), kind=kCustom, calls=%fused_computation.2 | custom fusion | bytes 262144 | tf_op jit(solution)/shard_map/vmap()/gather | solution.py:49
  434.0 34.1 %copy.129 = bf16[4,6,8,8,64,64]{4,3,5,2,1,0:T(8,128)(2,1)} copy(bf16[4,6,8,8,64,64]{5,4,1,3,2,0:T(8,128)(2,1)} %bitcast.232) | data formatting | bytes 25165824 | tf_op jit(solution)/shard_map/vmap()/gather | solution.py:55
  468.1 33.1 %reshape.459 = bf16[4,6,8,512,64]{3,4,2,1,0:T(8,128)(2,1)} reshape(bf16[4,6,8,8,64,64]{4,3,5,2,1,0:T(8,128)(2,1)} %copy.129) | data formatting | bytes 25165824 | tf_op jit(solution)/shard_map/reshape | solution.py:56
  539.6 34.1 %copy.132 = bf16[4,6,8,8,64,64]{4,3,5,2,1,0:T(8,128)(2,1)} copy(bf16[4,6,8,8,64,64]{5,4,1,3,2,0:T(8,128)(2,1)} %bitcast.231) | data formatting | bytes 25165824 | tf_op jit(solution)/shard_map/vmap()/gather | solution.py:55
  573.8 33.1 %reshape.461 = bf16[4,6,8,512,64]{3,4,2,1,0:T(8,128)(2,1)} reshape(bf16[4,6,8,8,64,64]{4,3,5,2,1,0:T(8,128)(2,1)} %copy.132) | data formatting | bytes 25165824 | tf_op jit(solution)/shard_map/reshape | solution.py:56
  657.2 37.7 %conditional.2 = (bf16[4,128,384]{1,2,0:T(8,128)(2,1)S(1)}, f32[4,6,128,1]{2,1,0,3:T(8,128)S(1)}) conditional(s32[]{:T(128)} %convert_element_type.221, () %tuple.24, (pred[4,1,128,2048]{3,2,0,1:T(8,128)(4,1)S(1)}, bf16[4,6,128,64]{2,0,3,1:T(4,128)(2,1)S(1)}, bf16[4,6,2048,64]{2,3,1,0:T(8,128)(2,1)}, bf16[4,6,2048,64]{2,3,1,0:T(8,128)(2,1)}) %tuple.114), branch_computations={%region_0.1_spmd, %region_1.0_spmd} | conditional | flops 1686303744 | bytes 92110864 | solution.py:236
  705.8 152.3 %all-reduce.9.cloned.1.call-done = f32[2048,768]{1,0:T(8,128)} async-done(((f32[2048,768]{1,0:T(8,128)}), f32[2048,768]{1,0:T(8,128)}) %all-reduce.9.cloned.1.call-update) | async-done | bytes 6291472 | tf_op jit(solution)/shard_map/psum | solution.py:240
  890.7 152.7 %all-reduce.11.cloned.1.call-done = f32[2048,768]{1,0:T(8,128)} async-done(((f32[2048,768]{1,0:T(8,128)}), f32[2048,768]{1,0:T(8,128)}) %all-reduce.11.cloned.1.call-update) | async-done | bytes 6291472 | tf_op jit(solution)/shard_map/psum | solution.py:251
  1091.0 151.8 %all-reduce.13.cloned.1.call-done = f32[2048,768]{1,0:T(8,128)} async-done(((f32[2048,768]{1,0:T(8,128)}), f32[2048,768]{1,0:T(8,128)}) %all-reduce.13.cloned.1.call-update) | async-done | bytes 6291472 | tf_op jit(solution)/shard_map/psum | solution.py:266
  1272.0 26.1 %multiply_reduce_fusion.1 = (f32[4,6,8,64]{3,2,1,0:T(8,128)S(1)}, f32[4,6,8,64,512]{4,3,2,1,0:T(8,128)}) fusion(f32[4,6,8,64,512]{4,3,2,1,0:T(8,128)} %get-tuple-element.216, f32[4,6,8,64]{3,2,1,0:T(8,128)} %log_add_fusion, bf16[4,6,8,512,64]{3,4,2,1,0:T(8,128)(2,1)} %reshape.461, bf16[4,6,8,64,64]{3,2,0,4,1:T(8,128)(2,1)S(1)} %reshape.533), kind=kOutput, calls=%fused_computation.36 | convolution fusion | flops 824168448 | bytes 64585728 | tf_op jit(solution)/shard_map/shnqd,shnkd->shnqk/dot_general | solution.py:286
  1336.3 24.8 %copy.143 = f32[4,6,8,512,64]{3,2,4,1,0:T(8,128)} copy(f32[4,6,8,512,64]{3,4,2,1,0:T(8,128)} %broadcast_multiply_fusion.1) | data formatting | bytes 50331648 | tf_op jit(solution)/shard_map/mul | solution.py:341
  1361.1 36.4 %reshape.472 = f32[4,6,64,64,64]{3,2,4,1,0:T(8,128)} reshape(f32[4,6,8,512,64]{3,2,4,1,0:T(8,128)} %copy.143) | data formatting | bytes 50331648 | tf_op jit(solution)/shard_map/reshape | solution.py:109
  1397.5 48.9 %copy.157 = f32[4,64,6,64,64]{4,3,2,1,0:T(8,128)} copy(f32[4,64,6,64,64]{3,1,4,2,0:T(8,128)} %bitcast.222) | data formatting | bytes 50331648 | tf_op jit(solution)/shard_map/reshape | solution.py:109
  1458.0 125.0 %scatter_fusion = f32[4,6,32,64,64]{4,3,2,1,0:T(8,128)} fusion(f32[4,6,32,64,64]{4,3,2,1,0:T(8,128)} %broadcast.500.clone, s32[256]{0:T(256)S(1)} %reshape.510, f32[256,6,64,64]{3,2,1,0:T(8,128)} %bitcast.225), kind=kCustom, calls=%fused_computation.5 | custom fusion | flops 6291456 | bytes 75499520 | tf_op jit(solution)/shard_map/vmap()/scatter-add | solution.py:111
  1601.8 92.1 %conditional.3 = (bf16[4,128,384]{1,2,0:T(8,128)(2,1)S(1)}, f32[4,2048,384]{1,2,0:T(8,128)}, f32[4,2048,384]{1,2,0:T(8,128)}) conditional(s32[]{:T(128)} %convert_element_type.221, () %tuple.26, (pred[4,1,128,2048]{3,2,0,1:T(8,128)(4,1)S(1)}, bf16[4,6,128,64]{2,0,3,1:T(4,128)(2,1)S(1)}, bf16[4,6,2048,64]{2,3,1,0:T(8,128)(2,1)}, ...), branch_computations={%region_17.18_spmd, %region_18.20_spmd} | conditional | flops 4124439552 | bytes 237957152 | solution.py:333
  1729.6 24.8 %copy.149 = f32[4,6,8,512,64]{3,2,4,1,0:T(8,128)} copy(f32[4,6,8,512,64]{3,4,2,1,0:T(8,128)} %fusion.29) | data formatting | bytes 50331648 | tf_op jit(solution)/shard_map/shnqk,shnqd->shnkd/dot_general | solution.py:334
  1754.4 36.4 %reshape.475 = f32[4,6,64,64,64]{3,2,4,1,0:T(8,128)} reshape(f32[4,6,8,512,64]{3,2,4,1,0:T(8,128)} %copy.149) | data formatting | bytes 50331648 | tf_op jit(solution)/shard_map/reshape | solution.py:109
  1790.8 48.9 %copy.158 = f32[4,64,6,64,64]{4,3,2,1,0:T(8,128)} copy(f32[4,64,6,64,64]{3,1,4,2,0:T(8,128)} %bitcast.223) | data formatting | bytes 50331648 | tf_op jit(solution)/shard_map/reshape | solution.py:109
  1851.3 125.0 %scatter_fusion.1 = f32[4,6,32,64,64]{4,3,2,1,0:T(8,128)} fusion(f32[4,6,32,64,64]{4,3,2,1,0:T(8,128)} %broadcast.500.clone.1, s32[256]{0:T(256)S(1)} %copy-done.6, f32[256,6,64,64]{3,2,1,0:T(8,128)} %bitcast.224), kind=kCustom, calls=%fused_computation.6 | custom fusion | flops 6291456 | bytes 75499520 | tf_op jit(solution)/shard_map/vmap()/scatter-add | solution.py:111
  2136.0 47.1 %reduce-scatter.23.cloned.1.call-done = bf16[1536,192]{0,1:T(8,128)(2,1)} async-done(((bf16[1536,768]{0,1:T(8,128)(2,1)}), bf16[1536,192]{0,1:T(8,128)(2,1)}) %reduce-scatter.23.cloned.1.call-update) | async-done | bytes 589840 | tf_op jit(solution)/shard_map/reduce_scatter | solution.py:435
  2183.1 49.8 %reduce-scatter.21.cloned.1.call-done = bf16[192,1536]{1,0:T(8,128)(2,1)} async-done(((bf16[768,1536]{1,0:T(8,128)(2,1)}), bf16[192,1536]{1,0:T(8,128)(2,1)}) %reduce-scatter.21.cloned.1.call-update) | async-done | bytes 589840 | tf_op jit(solution)/shard_map/reduce_scatter | solution.py:432
  2284.5 59.2 %all-reduce.1 = (f32[384]{0:T(512)}, f32[384]{0:T(512)}, f32[768]{0:T(1024)}, f32[768]{0:T(1024)}, f32[768]{0:T(1024)}, /*index=5*/f32[1536]{0:T(1024)}, f32[768...) all-reduce(f32[384]{0:T(512)S(1)} %get-tuple-element.193, ...), channel_id=1, replica_groups=mesh['dp'=4,'context'=4,'tensor'=2] {'dp','context'}, use_global_device_ids=true, to_apply=%region_29.30 | all-reduce | flops 6918 | bytes 55344 | tf_op jit(solution)/shard_map/psum | solution.py:403
  2356.8 40.5 %all-reduce.15.cloned.1.call-done = bf16[2048,768]{1,0:T(8,128)(2,1)} async-done(((bf16[2048,768]{1,0:T(8,128)(2,1)}), bf16[2048,768]{1,0:T(8,128)(2,1)}) %all-reduce.15.cloned.1.call-update) | async-done | bytes 3145744 | tf_op jit(solution)/shard_map/psum | solution.py:372
  (378 shorter events, 833.3 us)
Async XLA Ops:
  8.1 386.9 %all-gather.5.cloned.1.call-start = ((), (), s32[]{:S(2)}) async-start(), calls=%async_computation.8 | async-start | bytes 7864320 | tf_op jit(solution)/shard_map/all_gather | solution.py:171
  32.3 468.8 %all-gather.7.cloned.1.call-start = ((), (), s32[]{:S(2)}) async-start(), calls=%async_computation.9 | async-start | bytes 7864320 | tf_op jit(solution)/shard_map/all_gather | solution.py:174
  52.5 805.6 %all-reduce.9.cloned.1.call-start = ((), (), s32[]{:S(2)}) async-start(), calls=%async_computation.10 | async-start | bytes 12582912 | tf_op jit(solution)/shard_map/psum | solution.py:240
  237.6 156.2 %slice-start = ((s32[4,2048]{1,0:T(4,128)}), s32[4,128]{1,0:T(4,128)S(1)}, s32[]{:S(2)}) async-start(s32[4,2048]{1,0:T(4,128)} %param.26), calls=%async_computation.25 | async-start | bytes 4096 | tf_op jit(solution)/shard_map/slice | solution.py:91
  394.9 262.2 %copy-start.9 = (pred[4,1,128,2048]{3,2,0,1:T(8,128)(4,1)}, pred[4,1,128,2048]{3,2,0,1:T(8,128)(4,1)S(1)}, u32[]{:S(2)}) copy-start(pred[4,1,128,2048]{3,2,0,1:T(8,128)(4,1)S(1)} %and_or_fusion) | copy-start | bytes 3145732
  704.5 161.9 %all-gather.9.cloned.1.call-start = ((), (), s32[]{:S(2)}) async-start(), calls=%async_computation.11 | async-start | bytes 2949120 | tf_op jit(solution)/shard_map/all_gather | solution.py:156
  705.1 175.2 %all-gather.11.cloned.1.call-start = ((), (), s32[]{:S(2)}) async-start(), calls=%async_computation.12 | async-start | bytes 2949120 | tf_op jit(solution)/shard_map/all_gather | solution.py:157
  705.7 337.7 %all-reduce.11.cloned.1.call-start = ((), (), s32[]{:S(2)}) async-start(), calls=%async_computation.13 | async-start | bytes 12582912 | tf_op jit(solution)/shard_map/psum | solution.py:251
  705.7 545.9 %copy-start.53 = (f32[768]{0:T(1024)}, f32[768]{0:T(1024)S(1)}, u32[]{:S(2)}) copy-start(f32[768]{0:T(1024)S(1)} %convert_element_type.230) | copy-start | bytes 9220
  705.8 337.6 %copy-start.64 = (f32[768]{0:T(1024)}, f32[768]{0:T(1024)S(1)}, u32[]{:S(2)}) copy-start(f32[768]{0:T(1024)S(1)} %convert_element_type.231) | copy-start | bytes 9220
  862.9 388.8 %copy-start.44 = (f32[2048]{0:T(1024)}, f32[2048]{0:T(1024)S(1)}, u32[]{:S(2)}) copy-start(f32[2048]{0:T(1024)S(1)} %broadcast_multiply_fusion.5) | copy-start | bytes 24580
  866.3 385.4 %copy-start.48 = (f32[2048]{0:T(1024)}, f32[2048]{0:T(1024)S(1)}, u32[]{:S(2)}) copy-start(f32[2048]{0:T(1024)S(1)} %fusion.59) | copy-start | bytes 24580
  890.0 352.8 %all-reduce.13.cloned.1.call-start = ((), (), s32[]{:S(2)}) async-start(), calls=%async_computation.14 | async-start | bytes 12582912 | tf_op jit(solution)/shard_map/psum | solution.py:266
  1089.4 945.0 %reduce-scatter.15.cloned.1.call-start = ((), (), s32[]{:S(2)}) async-start(), calls=%async_computation.15 | async-start | bytes 7864320 | tf_op jit(solution)/shard_map/reduce_scatter | solution.py:348
  1090.3 367.7 %copy-start.5 = (s32[256]{0:T(256)}, s32[256]{0:T(256)S(1)}, u32[]{:S(2)}) copy-start(s32[256]{0:T(256)S(1)} %reshape.510) | copy-start | bytes 3076
  1706.4 357.5 %reduce-scatter.17.cloned.1.call-start = ((), (), s32[]{:S(2)}) async-start(), calls=%async_computation.16 | async-start | bytes 7864320 | tf_op jit(solution)/shard_map/reduce_scatter | solution.py:351
  2006.8 96.5 %reduce-scatter.25.cloned.1.call-start = ((), (), s32[]{:S(2)}) async-start(), calls=%async_computation.21 | async-start | bytes 737280
  2034.4 77.3 %reduce-scatter.27.cloned.1.call-start = ((), (), s32[]{:S(2)}) async-start(), calls=%async_computation.22 | async-start | bytes 737280
  2040.3 94.0 %reduce-scatter.29.cloned.1.call-start = ((), (), s32[]{:S(2)}) async-start(), calls=%async_computation.23 | async-start | bytes 737280
  2069.7 113.4 %reduce-scatter.23.cloned.1.call-start = ((), (), s32[]{:S(2)}) async-start(), calls=%async_computation.20 | async-start | bytes 2949120 | tf_op jit(solution)/shard_map/reduce_scatter | solution.py:435
  2079.4 153.5 %reduce-scatter.21.cloned.1.call-start = ((), (), s32[]{:S(2)}) async-start(), calls=%async_computation.19 | async-start | bytes 2949120 | tf_op jit(solution)/shard_map/reduce_scatter | solution.py:432
  2091.9 165.5 %reduce-scatter.19.cloned.1.call-start = ((), (), s32[]{:S(2)}) async-start(), calls=%async_computation.18 | async-start | bytes 737280 | tf_op jit(solution)/shard_map/reduce_scatter | solution.py:429
  2096.6 248.8 %all-reduce.17.cloned.1.call-start = ((), (), s32[]{:S(2)}) async-start(), calls=%async_computation.24 | async-start | bytes 3833856 | tf_op jit(solution)/shard_map/psum | solution.py:440
  2257.4 139.9 %all-reduce.15.cloned.1.call-start = ((), (), s32[]{:S(2)}) async-start(), calls=%async_computation.17 | async-start | bytes 6291456 | tf_op jit(solution)/shard_map/psum | solution.py:372
  (73 other events, 1178.8 us)
Sparse Core Ops, SparseCore 0:
  32.5 47.7 all-gather.4
  82.4 46.3 all-gather.6
  704.6 153.4 all-reduce.8
  890.1 153.1 all-reduce.10
  1089.5 153.1 all-reduce.12
  1706.6 57.3 reduce-scatter.14
  2006.9 56.9 reduce-scatter.16
  2066.9 21.9 reduce-scatter.24
  2091.3 20.3 reduce-scatter.26
  2113.9 20.3 reduce-scatter.28
  2136.7 46.3 reduce-scatter.22
  2185.4 47.5 reduce-scatter.20
  2235.9 21.4 reduce-scatter.18
  2260.8 48.3 all-reduce.16
  2311.4 85.8 all-reduce.14
Sparse Core Ops, SparseCore 1:
  706.6 50.2 all-gather.8
  758.4 48.6 all-gather.10
where the time goes:
time: 2430 us; the launch traced here: 2410 us
  local copies, waits for them, and re-layouts  861 us (35%)
  waiting for transfers between devices  670 us (28%)
  other arithmetic  406 us (17%)
  matrix products  329 us (14%)
  blocking collectives  126 us (5%)
    gather x6, local copies, waits for them, and re-layouts, pick_rows(): one_table[one_index]  294 us
    scatter-add x3, other arithmetic, place_tiles(): acc_one.at[:, ids_one].add(vals_one)  250 us
    reshape x4, local copies, waits for them, and re-layouts, place_tiles(): grad_sel.reshape(seq_count, heads_local, slot_total, block_len, head_size)  171 us
    psum x1, waiting for transfers between devices, local(): ffn_out = lax.psum(ffn_part, 'tensor') + down_bias.astype(jnp.float32)  153 us
    psum x1, waiting for transfers between devices, local(): attn_out = lax.psum(attn_part, 'tensor') + output_bias.astype(jnp.float32)  152 us
    psum x1, waiting for transfers between devices, local(): lax.psum(jnp.dot(g_pre, w_up.T, preferred_element_type=jnp.float32), 'ten...  152 us
    gather x5, local copies, waits for them, and re-layouts, pick_tiles(): one_table[:, one_index]  104 us
    reshape x2, local copies, waits for them, and re-layouts, pick_tiles(): picked.reshape(seq_count, heads_local, local_blocks, slot_count * block_l...  66.2 us
  transfers between devices with their start and end apart: 17, of which 10 were waited for; matrix products, arithmetic and copies ran while one was open for 35% of the time, Pallas kernels for 0%

commit v1 on v0

v1 whole, which is shorter than its diff:
```python
import jax
import jax.numpy as jnp
from jax import lax
from jax.experimental import pallas as pl
from jax.experimental.pallas import tpu as pltpu
from jax.sharding import PartitionSpec as P

HD = 64
BLK = 64
PAIR = 128
SLOTS = 8
WIDE = 512
SCALE = HD ** (-0.5)
EPSILON = 1e-06


NEG_FILL = -1e30


def pair_rows(block, left, scale=None):
    if scale is not None:
        block = block * jnp.asarray(scale, block.dtype)
    zero = jnp.zeros_like(block)
    return jnp.concatenate([jnp.where(left, block, zero), jnp.where(left, zero, block)], 0)


def lane_left(rows):
    return lax.broadcasted_iota(jnp.int32, (rows, PAIR), 1) < HD


def eye_pair():
    lanes = lax.broadcasted_iota(jnp.int32, (BLK, PAIR), 1)
    rows = lax.broadcasted_iota(jnp.int32, (BLK, PAIR), 0)
    return rows == lanes % BLK


def block_rows(index):
    return pl.ds(pl.multiple_of(index * BLK, BLK), BLK)


def slot_bias(table, row, key_code, query_code, own):
    pieces = []
    for slot in range(SLOTS):
        code = query_code
        if slot == 0:
            code = jnp.where(table[row, 9] == 1, query_code, -2)
        if slot == 2:
            code = jnp.where(table[row, 10] == 1, query_code, -2)
        same = key_code[block_rows(table[row, 1 + slot]), :] == code
        if slot == 1:
            same = same | own
        pieces.append(jnp.where(same, 0.0, NEG_FILL))
    return jnp.concatenate(pieces, 0)


def slot_rows(ref, table, row, lanes):
    return jnp.concatenate(
        [ref[block_rows(table[row, 1 + slot]), lanes] for slot in range(SLOTS)], 0
    )


def wide_bias(key_code, query_code, block, chunk):
    start = pl.multiple_of(chunk * WIDE, WIDE)
    same = key_code[pl.ds(start, WIDE), :] == query_code
    key_pos = start + lax.broadcasted_iota(jnp.int32, (WIDE, PAIR), 0)
    query_pos = block * BLK + lax.broadcasted_iota(jnp.int32, (WIDE, PAIR), 1) % BLK
    return jnp.where(same | (key_pos == query_pos), 0.0, NEG_FILL)


def dot_nt(left, right):
    return lax.dot_general(
        left, right, (((1,), (1,)), ((), ())), preferred_element_type=jnp.float32
    )


def dot_tn(left, right):
    return lax.dot_general(
        left, right, (((0,), (0,)), ((), ())), preferred_element_type=jnp.float32
    )


def dot_nn(left, right):
    return jnp.dot(left, right, preferred_element_type=jnp.float32)


def attend_kernel(table, wide, q_ref, k_ref, v_ref, key_code, query_code, o_ref, lse_ref, acc):
    length, width = q_ref.shape
    pairs = width // PAIR
    left = lane_left(BLK)
    own = eye_pair()

    def narrow(row, carry):
        block = table[row, 0]
        rows = block_rows(block)
        bias = slot_bias(table, row, key_code, query_code[pl.ds(block, 1), :], own)
        for pair in range(pairs):
            lanes = slice(pair * PAIR, (pair + 1) * PAIR)
            query = pair_rows(q_ref[rows, lanes], left, SCALE)
            scores = dot_nt(slot_rows(k_ref, table, row, lanes), query) + bias
            top = jnp.max(scores, 0, keepdims=True)
            weight = jnp.exp(scores - top)
            total = jnp.sum(weight, 0, keepdims=True)
            probs = (weight * (1.0 / total)).astype(jnp.bfloat16)
            lse_ref[block, pl.ds(pair, 1), :] = top + jnp.log(total)
            both = dot_tn(probs, slot_rows(v_ref, table, row, lanes))
            o_ref[rows, lanes] = jnp.where(left, both[:BLK], both[BLK:]).astype(o_ref.dtype)
        return carry

    lax.fori_loop(0, table.shape[0], narrow, 0)

    for which in range(2):
        block = wide[which]
        rows = block_rows(block)
        code = query_code[pl.ds(block, 1), :]

        def first(chunk, carry):
            bias = wide_bias(key_code, code, block, chunk)
            keys = pl.ds(pl.multiple_of(chunk * WIDE, WIDE), WIDE)
            out = []
            for pair in range(pairs):
                lanes = slice(pair * PAIR, (pair + 1) * PAIR)
                query = pair_rows(q_ref[rows, lanes], left, SCALE)
                scores = dot_nt(k_ref[keys, lanes], query) + bias
                top_old, total_old = carry[pair]
                top = jnp.maximum(top_old, jnp.max(scores, 0, keepdims=True))
                total = total_old * jnp.exp(top_old - top) + jnp.sum(
                    jnp.exp(scores - top), 0, keepdims=True
                )
                out.append((top, total))
            return tuple(out)

        start = (jnp.full((1, PAIR), NEG_FILL), jnp.zeros((1, PAIR), jnp.float32))
        ends = lax.fori_loop(0, length // WIDE, first, (start,) * pairs)
        for pair in range(pairs):
            lse_ref[block, pl.ds(pair, 1), :] = ends[pair][0] + jnp.log(ends[pair][1])
        acc[...] = jnp.zeros_like(acc)

        def second(chunk, carry):
            bias = wide_bias(key_code, code, block, chunk)
            keys = pl.ds(pl.multiple_of(chunk * WIDE, WIDE), WIDE)
            for pair in range(pairs):
                lanes = slice(pair * PAIR, (pair + 1) * PAIR)
                query = pair_rows(q_ref[rows, lanes], left, SCALE)
                scores = dot_nt(k_ref[keys, lanes], query) + bias
                probs = jnp.exp(scores - lse_ref[block, pl.ds(pair, 1), :]).astype(jnp.bfloat16)
                acc[pair] += dot_tn(probs, v_ref[keys, lanes])
            return carry

        lax.fori_loop(0, length // WIDE, second, 0)
        for pair in range(pairs):
            lanes = slice(pair * PAIR, (pair + 1) * PAIR)
            both = acc[pair]
            o_ref[rows, lanes] = jnp.where(left, both[:BLK], both[BLK:]).astype(o_ref.dtype)


def attend_back_kernel(
    table, wide, q_ref, k_ref, v_ref, do_ref, key_code, query_code, lse_ref,
    dq_ref, dk_ref, dv_ref, dk_sum, dv_sum, dq_acc,
):
    length, width = q_ref.shape
    pairs = width // PAIR
    left = lane_left(BLK)
    own = eye_pair()
    dk_sum[...] = jnp.zeros_like(dk_sum)
    dv_sum[...] = jnp.zeros_like(dv_sum)

    def narrow(row, carry):
        block = table[row, 0]
        rows = block_rows(block)
        bias = slot_bias(table, row, key_code, query_code[pl.ds(block, 1), :], own)
        for pair in range(pairs):
            lanes = slice(pair * PAIR, (pair + 1) * PAIR)
            query = pair_rows(q_ref[rows, lanes], left, SCALE)
            grad = pair_rows(do_ref[rows, lanes], left)
            keys = slot_rows(k_ref, table, row, lanes)
            values = slot_rows(v_ref, table, row, lanes)
            scores = dot_nt(keys, query) + bias
            probs = jnp.exp(scores - lse_ref[block, pl.ds(pair, 1), :])
            g_probs = dot_nt(values, grad)
            terms = probs * g_probs
            g_scores = (terms - probs * jnp.sum(terms, 0, keepdims=True)).astype(jnp.bfloat16)
            dv = dot_nn(probs.astype(jnp.bfloat16), grad)
            dk = dot_nn(g_scores, query)
            both = dot_tn(g_scores, keys)
            dq_ref[rows, lanes] = (jnp.where(left, both[:BLK], both[BLK:]) * SCALE).astype(
                dq_ref.dtype
            )
            for slot in range(SLOTS):
                spot = block_rows(table[row, 1 + slot])
                part = slice(slot * BLK, (slot + 1) * BLK)
                dk_sum[spot, lanes] += dk[part]
                dv_sum[spot, lanes] += dv[part]
        return carry

    lax.fori_loop(0, table.shape[0], narrow, 0)

    for which in range(2):
        block = wide[which]
        rows = block_rows(block)
        code = query_code[pl.ds(block, 1), :]

        def pieces(chunk, pair, bias):
            keys_at = pl.ds(pl.multiple_of(chunk * WIDE, WIDE), WIDE)
            lanes = slice(pair * PAIR, (pair + 1) * PAIR)
            query = pair_rows(q_ref[rows, lanes], left, SCALE)
            grad = pair_rows(do_ref[rows, lanes], left)
            keys = k_ref[keys_at, lanes]
            scores = dot_nt(keys, query) + bias
            probs = jnp.exp(scores - lse_ref[block, pl.ds(pair, 1), :])
            return keys_at, lanes, query, grad, keys, probs, probs * dot_nt(v_ref[keys_at, lanes], grad)

        def first(chunk, carry):
            bias = wide_bias(key_code, code, block, chunk)
            return tuple(
                carry[pair] + jnp.sum(pieces(chunk, pair, bias)[-1], 0, keepdims=True)
                for pair in range(pairs)
            )

        deltas = lax.fori_loop(
            0, length // WIDE, first, (jnp.zeros((1, PAIR), jnp.float32),) * pairs
        )
        dq_acc[...] = jnp.zeros_like(dq_acc)

        def second(chunk, carry):
            bias = wide_bias(key_code, code, block, chunk)
            for pair in range(pairs):
                keys_at, lanes, query, grad, keys, probs, terms = pieces(chunk, pair, bias)
                g_scores = (terms - probs * carry[pair]).astype(jnp.bfloat16)
                dv_sum[keys_at, lanes] += dot_nn(probs.astype(jnp.bfloat16), grad)
                dk_sum[keys_at, lanes] += dot_nn(g_scores, query)
                dq_acc[pair] += dot_tn(g_scores, keys)
            return carry

        lax.fori_loop(0, length // WIDE, second, deltas)
        for pair in range(pairs):
            lanes = slice(pair * PAIR, (pair + 1) * PAIR)
            both = dq_acc[pair]
            dq_ref[rows, lanes] = (jnp.where(left, both[:BLK], both[BLK:]) * SCALE).astype(
                dq_ref.dtype
            )
    dk_ref[...] = dk_sum[...].astype(dk_ref.dtype)
    dv_ref[...] = dv_sum[...].astype(dv_ref.dtype)


VMEM_SPEC = pl.BlockSpec(memory_space=pltpu.VMEM)
SMEM_SPEC = pl.BlockSpec(memory_space=pltpu.SMEM)
ROOM = pltpu.CompilerParams(vmem_limit_bytes=60 * 1024 * 1024)


def attend(table, wide, q, k, v, key_code, query_code):
    length, width = q.shape
    return pl.pallas_call(
        attend_kernel,
        out_shape=(
            jax.ShapeDtypeStruct((length, width), jnp.bfloat16),
            jax.ShapeDtypeStruct((length // BLK, 8, PAIR), jnp.float32),
        ),
        in_specs=[SMEM_SPEC] * 2 + [VMEM_SPEC] * 5,
        out_specs=(VMEM_SPEC, VMEM_SPEC),
        scratch_shapes=[pltpu.VMEM((width // PAIR, PAIR, PAIR), jnp.float32)],
        compiler_params=ROOM,
        cost_estimate=pl.CostEstimate(
            flops=length * width * 1024 * 6, bytes_accessed=length * width * 8,
            transcendentals=length * width * 8,
        ),
        name="attend",
    )(table, wide, q, k, v, key_code, query_code)


def attend_back(table, wide, q, k, v, do, key_code, query_code, lse):
    length, width = q.shape
    shape = jax.ShapeDtypeStruct((length, width), jnp.bfloat16)
    return pl.pallas_call(
        attend_back_kernel,
        out_shape=(shape, shape, shape),
        in_specs=[SMEM_SPEC] * 2 + [VMEM_SPEC] * 7,
        out_specs=(VMEM_SPEC,) * 3,
        scratch_shapes=[
            pltpu.VMEM((length, width), jnp.float32),
            pltpu.VMEM((length, width), jnp.float32),
            pltpu.VMEM((width // PAIR, PAIR, PAIR), jnp.float32),
        ],
        compiler_params=ROOM,
        cost_estimate=pl.CostEstimate(
            flops=length * width * 1024 * 15, bytes_accessed=length * width * 14,
            transcendentals=length * width * 8,
        ),
        name="attend_back",
    )(table, wide, q, k, v, do, key_code, query_code, lse)


def layer_norm(values, norm_gain, norm_shift):
    row_mean = jnp.mean(values, -1, keepdims=True)
    centered = values - row_mean
    row_var = jnp.mean(centered * centered, -1, keepdims=True)
    return centered * lax.rsqrt(row_var + EPSILON) * norm_gain + norm_shift


def gelu_tanh(values):
    return jax.nn.gelu(values, approximate=True)


def block_tables(random_seq, all_blocks, place):
    block = jnp.arange(2, all_blocks, dtype=jnp.int32)
    last = all_blocks - 1
    zero = jnp.zeros_like(block)
    true_ids = jnp.stack(
        [block, block - 1, block, jnp.minimum(block + 1, last), zero, zero + 1], -1
    )
    true_ids = jnp.concatenate([true_ids, random_seq[2:]], -1)
    flags = jnp.stack([block >= 3, block <= last - 1], -1).astype(jnp.int32)
    return (
        jnp.concatenate([place(true_ids), flags], -1).astype(jnp.int32),
        place(jnp.arange(2, dtype=jnp.int32)),
    )


def local(
    hidden_in, out_grad, segment_ids, token_valid, random_blocks,
    query_weight, query_bias, key_weight, value_weight, value_bias,
    output_weight, output_bias, norm1_gain, norm1_shift,
    up_weight, up_bias, down_weight, down_bias, norm2_gain, norm2_shift,
):
    f32, bf16 = jnp.float32, jnp.bfloat16
    seqs, span, width = hidden_in.shape
    length = segment_ids.shape[1]
    places = length // span
    halves = lax.axis_size("tensor")
    turns = seqs // halves
    shares = places // turns
    my_half = lax.axis_index("tensor")
    my_place = lax.axis_index("context")
    my_turn, my_share = my_place // shares, my_place % shares
    my_seq = my_half * turns + my_turn
    blocks = length // BLK
    rows = turns * span
    everyone = ("dp", "context", "tensor")

    def send_turn(value, step):
        if step % turns == 0:
            return value
        pairs = [
            (t * shares + s, ((t + step) % turns) * shares + s)
            for t in range(turns)
            for s in range(shares)
        ]
        return lax.ppermute(value, "context", pairs)

    def send_share(value, step):
        if step % shares == 0:
            return value
        pairs = [
            (t * shares + s, t * shares + (s + step) % shares)
            for t in range(turns)
            for s in range(shares)
        ]
        return lax.ppermute(value, "context", pairs)

    def bring(value):
        return jnp.concatenate(
            [
                send_turn(
                    lax.dynamic_index_in_dim(
                        value, my_half * turns + (my_turn + k) % turns, 0, keepdims=False
                    ),
                    k,
                )
                for k in range(turns)
            ],
            0,
        )

    def deliver(value):
        value = value.reshape(turns, span, width)
        got = jnp.stack([send_turn(value[k], -k) for k in range(turns)])
        order = (jnp.arange(turns) - my_turn) % turns
        got = jnp.stack(
            [lax.dynamic_index_in_dim(got, order[t], 0, keepdims=False) for t in range(turns)]
        )
        return lax.all_gather(got, "tensor", axis=0, tiled=True)

    def own_slice(value, count, which, axis):
        size = value.shape[axis] // count
        return lax.dynamic_slice_in_dim(value, which * size, size, axis)

    both = lambda w, a, b: lax.all_gather(
        lax.all_gather(w, "dp", axis=a, tiled=True), "tensor", axis=b, tiled=True
    )
    w_q, w_k, w_v = (both(w, 0, 1) for w in (query_weight, key_weight, value_weight))
    w_out = both(output_weight, 1, 0)
    w_up, w_down = both(up_weight, 0, 1), both(down_weight, 1, 0)
    b_q, b_v, b_up = (
        lax.all_gather(b, "tensor", axis=0, tiled=True) for b in (query_bias, value_bias, up_bias)
    )
    part = width // shares
    padded = -(-part // PAIR) * PAIR
    pad_cols = lambda w: jnp.pad(w, [(0, 0)] * (w.ndim - 1) + [(0, padded - part)])
    mine = lambda w: pad_cols(own_slice(w, shares, my_share, w.ndim - 1))
    w_qkv = jnp.concatenate([mine(w_q), mine(w_k), mine(w_v)], 1)
    b_qkv = jnp.concatenate([mine(b_q), jnp.zeros((padded,), bf16), mine(b_v)]).astype(f32)
    w_out_mine = jnp.concatenate(
        [own_slice(w_out, shares, (my_share + k) % shares, 0) for k in range(shares)], 0
    )

    x_own = bring(hidden_in)
    g_out = bring(out_grad).astype(f32)
    x_seq = jnp.concatenate([send_share(x_own, k) for k in range(shares)], 0)
    per = span // BLK

    def place(block_ids):
        chunk = block_ids // per
        turn, share = chunk // shares, chunk % shares
        spot = ((my_share - share) % shares) * turns + (my_turn - turn) % turns
        return spot * per + block_ids % per

    def in_order(row):
        return jnp.concatenate(
            [
                lax.dynamic_slice_in_dim(
                    row,
                    (((my_turn - k) % turns) * shares + (my_share - s) % shares) * span,
                    span,
                )
                for s in range(shares)
                for k in range(turns)
            ]
        )

    seg = in_order(lax.dynamic_index_in_dim(segment_ids, my_seq, 0, keepdims=False))
    live = in_order(lax.dynamic_index_in_dim(token_valid, my_seq, 0, keepdims=False))
    random_seq = lax.dynamic_index_in_dim(random_blocks, my_seq, 0, keepdims=False)
    table, wide = block_tables(random_seq, blocks, place)
    key_code = jnp.broadcast_to(jnp.where(live == 1, seg, -1)[:, None], (length, PAIR))
    query_code = jnp.tile(seg.reshape(blocks, BLK), (1, PAIR // BLK))

    qkv = (jnp.dot(x_seq, w_qkv, preferred_element_type=f32) + b_qkv).astype(bf16)
    q, k, v = (qkv[:, i * padded : (i + 1) * padded] for i in range(3))
    att, lse = attend(table, wide, q, k, v, key_code, query_code)
    att = att[:, :part].reshape(shares, rows, part)
    att_own = jnp.concatenate([send_share(att[s], -s) for s in range(shares)], 1)
    attn_out = jnp.dot(att_own, w_out_mine, preferred_element_type=f32) + output_bias.astype(f32)
    x_full = x_own.astype(f32)
    first_sum = x_full + attn_out
    gain_one, shift_one = norm1_gain.astype(f32), norm1_shift.astype(f32)
    normed = layer_norm(first_sum, gain_one, shift_one)
    normed_low = normed.astype(bf16)
    pre_act = jnp.dot(normed_low, w_up, preferred_element_type=f32) + b_up.astype(f32)
    act_low = gelu_tanh(pre_act).astype(bf16)
    ffn_out = jnp.dot(act_low, w_down, preferred_element_type=f32) + down_bias.astype(f32)
    second_sum = normed + ffn_out
    gain_two, shift_two = norm2_gain.astype(f32), norm2_shift.astype(f32)
    layer_out, norm_back = jax.vjp(layer_norm, second_sum, gain_two, shift_two)
    g_second, gain_two_grad, shift_two_grad = norm_back(g_out)
    layer_out = deliver(layer_out.astype(bf16))
    g_ffn = g_second.astype(bf16)
    g_act = jnp.dot(g_ffn, w_down.T, preferred_element_type=f32)
    g_pre = jax.vjp(gelu_tanh, pre_act)[1](g_act)[0].astype(bf16)
    up_part = jnp.dot(normed_low.T, g_pre, preferred_element_type=f32)
    down_part = jnp.dot(act_low.T, g_ffn, preferred_element_type=f32)
    g_normed = g_second + jnp.dot(g_pre, w_up.T, preferred_element_type=f32)
    g_first, gain_one_grad, shift_one_grad = jax.vjp(layer_norm, first_sum, gain_one, shift_one)[1](
        g_normed
    )
    g_attn = g_first.astype(bf16)
    out_part = jnp.dot(att_own.T, g_attn, preferred_element_type=f32).astype(bf16)
    g_att = jnp.dot(g_attn, w_out_mine.T, preferred_element_type=f32).astype(bf16)
    do = jnp.concatenate(
        [send_share(own_slice(g_att, shares, s, 1), s) for s in range(shares)], 0
    )
    dq, dk, dv = attend_back(table, wide, q, k, v, pad_cols(do), key_code, query_code, lse)
    dqkv = jnp.concatenate([dq, dk, dv], 1)
    qkv_part = jnp.dot(x_seq.T, dqkv, preferred_element_type=f32).astype(bf16)
    back = jnp.dot(dqkv, w_qkv.T, preferred_element_type=f32).reshape(shares, rows, width)
    back_own = back[0]
    for s in range(1, shares):
        back_own = back_own + send_share(back[s].astype(bf16), -s).astype(f32)
    input_grad = deliver((g_first + back_own).astype(bf16)).astype(f32)

    def spread(value, which, axis):
        shape = list(value.shape)
        size = shape[axis]
        shape[axis] = size * shares
        return lax.dynamic_update_slice_in_dim(
            jnp.zeros(shape, value.dtype), value, which * size, axis
        )

    def shard(value, dp_axis, tensor_axis):
        value = lax.psum_scatter(value, "tensor", scatter_dimension=tensor_axis, tiled=True)
        value = lax.psum_scatter(value, "dp", scatter_dimension=dp_axis, tiled=True)
        return lax.psum(value, "context").astype(f32)

    shard_q, shard_k, shard_v = (
        shard(spread(qkv_part[:, i * padded : i * padded + part], my_share, 1), 0, 1)
        for i in range(3)
    )
    out_full = jnp.concatenate(
        [own_slice(out_part, shares, (s - my_share) % shares, 0) for s in range(shares)], 0
    )
    shard_o = shard(out_full, 1, 0)
    shard_up = shard(up_part.astype(bf16), 0, 1)
    shard_down = shard(down_part.astype(bf16), 1, 0)

    sums = lambda value: jnp.sum(value.astype(f32), 0)
    valid = live[:rows].astype(f32)
    squares = lambda member: jnp.sum(valid * jnp.sum(member * member, -1))
    stats = jnp.stack(
        [squares(m) for m in (x_full, first_sum, second_sum, attn_out, ffn_out)] + [jnp.sum(valid)]
    )
    small = [
        spread(sums(dq)[:part], my_share, 0),
        spread(sums(dv)[:part], my_share, 0),
        sums(g_pre),
        sums(g_attn),
        gain_one_grad,
        shift_one_grad,
        sums(g_ffn),
        gain_two_grad,
        shift_two_grad,
        stats,
    ]
    small = lax.psum(tuple(small), everyone)
    s_q, s_v, s_up = (own_slice(value, halves, my_half, 0) for value in small[:3])
    s_o, s_g1, s_s1, s_down, s_g2, s_s2, stats = small[3:]
    input_rms = jnp.sqrt(stats[:5] / (jnp.maximum(stats[5], 1.0) * width))
    return (
        layer_out, input_grad, shard_q, s_q, shard_k, shard_v, s_v, shard_o, s_o,
        s_g1, s_s1, shard_up, s_up, shard_down, s_down, s_g2, s_s2, input_rms,
    )


def solution(mesh):
    rows, plain = P("dp", "context", None), P()
    columns, across, halves = P("dp", "tensor"), P("tensor", "dp"), P("tensor")
    return jax.shard_map(
        local,
        mesh=mesh,
        in_specs=(
            rows, rows, P("dp", None), P("dp", None), P("dp", None, None),
            columns, halves, columns, columns, halves, across, plain, plain, plain,
            columns, halves, across, plain, plain, plain,
        ),
        out_specs=(
            rows, rows, columns, halves, columns, columns, halves, across, plain,
            plain, plain, columns, halves, across, plain, plain, plain, plain,
        ),
        check_vma=False,
    )
```

time: 2430 us -> 999 us (0.41)
  local copies, waits for them, and re-layouts: 861 us -> 79.5 us
  other arithmetic: 406 us -> 33.4 us
  matrix products: 329 us -> 102 us
  waiting for transfers between devices: 670 us -> 508 us
  Pallas kernels: 0 us -> 96.1 us
    psum x5 -> x1, waiting for transfers between devices: 497 us -> 50 us  [shard(): return lax.psum(value, 'context').astype(f32)]
    gather x11 -> x0, local copies, waits for them, and re-layouts: 398 us -> none  [the longest x6 294 us: pick_rows(): one_table[one_index]]
    reshape x11 -> x0, local copies, waits for them, and re-layouts: 282 us -> none  [the longest x4 171 us: place_tiles(): grad_sel.reshape(seq_count, heads_local, slot_total, block_len, head_size)]
    scatter-add x3 -> x0, other arithmetic: 250 us -> none  [place_tiles(): acc_one.at[:, ids_one].add(vals_one)]
    dot_general x31 -> x12, matrix products: 329 us -> 102 us  [the longest x1 18.3 us: local(): g_act = jnp.dot(g_ffn, w_down.T, preferred_element_type=f32)]
    all_gather x4 -> x10, waiting for transfers between devices: 0.05 us -> 193 us  [the longest x6 150 us: local(): lax.all_gather(lax.all_gather(w, 'dp', axis=a, tiled=True), 'tensor', axi...]
    pallas_call x0 -> x2, Pallas kernels: none -> 96.1 us  [the longest x1 51.5 us: attend_back(): pl.pallas_call(attend_back_kernel, out_shape=(shape, shape, shape), in_sp...]
    convert_element_type x16 -> x15, other arithmetic: 73.3 us -> 15.2 us  [the longest x2 8.89 us: local(): input_grad = deliver((g_first + back_own).astype(bf16)).astype(f32)]
  transfers between devices with their start and end apart: 17 -> 31, of which waited for: 10 -> 18; matrix products, arithmetic and copies ran while one was open for 35% -> 16% of each run, Pallas kernels for 0% -> 10%
where the time goes in v1:
time: 999 us; the launch traced here: 989 us
  waiting for transfers between devices  508 us (51%)
  blocking collectives  143 us (14%)
  matrix products  102 us (10%)
  Pallas kernels  96.1 us (10%)
  local copies, waits for them, and re-layouts  79.5 us (8%)
  other arithmetic  33.4 us (3%)
  between operations  19.8 us (2%)
    all_gather x6, waiting for transfers between devices, local(): lax.all_gather(lax.all_gather(w, 'dp', axis=a, tiled=True), 'tensor', axi...  150 us
    reduce_scatter x4, waiting for transfers between devices, shard(): value = lax.psum_scatter(value, 'dp', scatter_dimension=dp_axis, tiled=True)  116 us
    all_gather x4, blocking collectives, local(): lax.all_gather(w, 'dp', axis=a, tiled=True)  87.5 us
    unnamed x28, waiting for transfers between devices  60.4 us
    reduce_scatter x3, waiting for transfers between devices, shard(): lax.psum_scatter(value, 'tensor', scatter_dimension=tensor_axis, tiled=True)  60.1 us
    pallas_call x1, Pallas kernels, attend_back(): pl.pallas_call(attend_back_kernel, out_shape=(shape, shape, shape), in_sp...  51.5 us
    psum x1, waiting for transfers between devices, shard(): return lax.psum(value, 'context').astype(f32)  50 us
    pallas_call x1, Pallas kernels, attend(): pl.pallas_call(attend_kernel, out_shape=(jax.ShapeDtypeStruct((length, wi...  44.6 us
  transfers between devices with their start and end apart: 31, of which 18 were waited for; matrix products, arithmetic and copies ran while one was open for 16% of the time, Pallas kernels for 10%

profile of v1, /device:TPU:0, one launch (start us, length us, event | category | flops | bytes accessed | tf_op | source)
XLA Modules:
  0.0 989.2 jit_solution(10929524735883614765)
XLA Ops:
  8.0 21.8 %all_gather.55 = bf16[768,384]{1,0:T(8,128)(2,1)} all-gather(bf16[192,384]{1,0:T(8,128)(2,1)} %param.28), channel_id=1, replica_groups=mesh['dp'=4,'context'=4,'tensor'=2] {'dp'}, dimensions={0}, use_global_device_ids=true | all-gather | bytes 737280 | tf_op jit(solution)/shard_map/all_gather | solution.py:387
  29.9 24.8 %all_gather.53 = bf16[768,384]{1,0:T(8,128)(2,1)} all-gather(bf16[192,384]{1,0:T(8,128)(2,1)} %param.27), channel_id=1, replica_groups=mesh['dp'=4,'context'=4,'tensor'=2] {'dp'}, dimensions={0}, use_global_device_ids=true | all-gather | bytes 737280 | tf_op jit(solution)/shard_map/all_gather | solution.py:387
  54.8 23.9 %all_gather.51 = bf16[768,384]{1,0:T(8,128)(2,1)} all-gather(bf16[192,384]{1,0:T(8,128)(2,1)S(1)} %copy-done.26), channel_id=1, replica_groups=mesh['dp'=4,'context'=4,'tensor'=2] {'dp'}, dimensions={0}, use_global_device_ids=true | all-gather | bytes 737280 | tf_op jit(solution)/shard_map/all_gather | solution.py:387
  79.3 17.0 %all_gather.59 = bf16[384,768]{0,1:T(8,128)(2,1)} all-gather(bf16[384,192]{0,1:T(8,128)(2,1)S(1)} %copy-done.27), channel_id=1, replica_groups=mesh['dp'=4,'context'=4,'tensor'=2] {'dp'}, dimensions={1}, use_global_device_ids=true | all-gather | bytes 737280 | tf_op jit(solution)/shard_map/all_gather | solution.py:387
  120.4 14.2 %all-gather.16.cloned.1.call-done = bf16[768,768]{1,0:T(8,128)(2,1)} async-done(((bf16[768,384]{1,0:T(8,128)(2,1)}), bf16[768,768]{1,0:T(8,128)(2,1)}) %all-gather.16.cloned.1.call-update) | async-done | bytes 1179664 | tf_op jit(solution)/shard_map/all_gather | solution.py:386
  136.6 22.3 %all-gather.14.cloned.1.call-done = bf16[768,768]{1,0:T(8,128)(2,1)} async-done(((bf16[768,384]{1,0:T(8,128)(2,1)}), bf16[768,768]{1,0:T(8,128)(2,1)}) %all-gather.14.cloned.1.call-update) | async-done | bytes 1179664 | tf_op jit(solution)/shard_map/all_gather | solution.py:386
  170.0 44.6 %attend.1 = (bf16[2048,384]{1,0:T(8,128)(2,1)}, f32[32,8,128]{2,1,0:T(8,128)}) custom-call(s32[30,11]{1,0:T(8,128)} %pad_add_fusion.table, s32[2]{0:T(128)} %get-tuple-element.199.wide, bf16[2048,384]{1,0:T(8,128)(2,1)} %get-tuple-element.152.q_ref, bf16[2048,384]{1,0:T(8,128)(2,1)} %get-tuple-element.151.k_ref, bf16[2048,384]{1,0:T(8,128)(2,1)} %get-tuple-element.150.v_ref, ...), custom_call_target="tpu_custom_call" | custom-call | flops 4831838208 | bytes 6291456 | tf_op jit(solution)/shard_map/attend/pallas_call | solution.py:252
  241.8 56.4 %all-gather.24.cloned.1.call-done = bf16[768,3072]{1,0:T(8,128)(2,1)} async-done(((bf16[768,1536]{1,0:T(8,128)(2,1)}), bf16[768,3072]{1,0:T(8,128)(2,1)}) %all-gather.24.cloned.1.call-update) | async-done | bytes 4718608 | tf_op jit(solution)/shard_map/all_gather | solution.py:386
  298.2 15.6 %multiply_convert_fusion = (bf16[1024,3072]{1,0:T(8,128)(2,1)}, f32[1024,3072]{1,0:T(8,128)}) fusion(f32[3072]{0:T(1024)S(1)} %bitcast.79, bf16[768,3072]{1,0:T(8,128)(2,1)} %all-gather.24.cloned.1.call-done, f32[1024,768]{0,1:T(8,128)} %copy-done.2, f32[768]{0:T(1024)S(1)} %convert_element_type.125, f32[768]{0:T(1024)S(1)} %convert_element_type.124, ...), kind=kOutput, calls=%fused_computation.10 | convolution fusion | flops 4867227648 | bytes 26765312 | tf_op jit(solution)/shard_map/dot_general | solution.py:447
  313.7 48.6 %all-gather.28.cloned.1.call-done = bf16[3072,768]{0,1:T(8,128)(2,1)} async-done(((bf16[1536,768]{0,1:T(8,128)(2,1)}), bf16[3072,768]{0,1:T(8,128)(2,1)}) %all-gather.28.cloned.1.call-update) | async-done | bytes 4718608 | tf_op jit(solution)/shard_map/all_gather | solution.py:386
  378.0 18.3 %convert_reduce_fusion = (f32[3072]{0:T(1024)S(1)}, bf16[1024,3072]{1,0:T(8,128)(2,1)}) fusion(f32[1024,3072]{1,0:T(8,128)} %get-tuple-element.194, f32[3072]{0:T(1024)S(1)} %bitcast.80, bf16[1024,768]{0,1:T(8,128)(2,1)S(1)} %get-tuple-element.133, bf16[3072,768]{0,1:T(8,128)(2,1)S(1)} %bitcast.90), kind=kOutput, calls=%fused_computation.9 | convolution fusion | flops 4904186880 | bytes 25190400 | tf_op jit(solution)/shard_map/dot_general | solution.py:456
  427.8 51.5 %attend_back.1 = (bf16[2048,384]{1,0:T(8,128)(2,1)}, bf16[2048,384]{1,0:T(8,128)(2,1)}, bf16[2048,384]{1,0:T(8,128)(2,1)}) custom-call(s32[30,11]{1,0:T(8,128)} %pad_add_fusion.table, s32[2]{0:T(128)} %get-tuple-element.199.wide, bf16[2048,384]{1,0:T(8,128)(2,1)} %get-tuple-element.152.q_ref, bf16[2048,384]{1,0:T(8,128)(2,1)} %get-tuple-element.151.k_ref, ...), custom_call_target="tpu_custom_call" | custom-call | flops 12079595520 | bytes 11010048 | tf_op jit(solution)/shard_map/attend_back/pallas_call | solution.py:273
  524.9 18.8 %reduce-scatter.39.cloned.1.call-done = bf16[384,768]{1,0:T(8,128)(2,1)} async-done(((bf16[768,768]{1,0:T(8,128)(2,1)}), bf16[384,768]{1,0:T(8,128)(2,1)}) %reduce-scatter.39.cloned.1.call-update) | async-done | bytes 589840
  545.9 21.8 %reduce-scatter.41.cloned.1.call-done = bf16[384,768]{1,0:T(8,128)(2,1)} async-done(((bf16[768,768]{1,0:T(8,128)(2,1)}), bf16[384,768]{1,0:T(8,128)(2,1)}) %reduce-scatter.41.cloned.1.call-update) | async-done | bytes 589840
  569.9 60.1 %reduce-scatter.31.cloned.1.call-done = bf16[768,1536]{1,0:T(8,128)(2,1)} async-done(((bf16[768,3072]{1,0:T(8,128)(2,1)}), bf16[768,1536]{1,0:T(8,128)(2,1)}) %reduce-scatter.31.cloned.1.call-update) | async-done | bytes 2359312 | tf_op jit(solution)/shard_map/reduce_scatter | solution.py:488
  665.4 16.7 %collective-permute-done.7 = bf16[512,768]{0,1:T(8,128)(2,1)S(1)} collective-permute-done((bf16[512,768]{0,1:T(8,128)(2,1)S(1)}, bf16[512,768]{0,1:T(8,128)(2,1)S(1)}, u32[]{:S(2)}, u32[]{:S(2)}) %collective-permute-start.7) | collective-permute-done | bytes 786464 | tf_op jit(solution)/shard_map/ppermute | solution.py:347
  686.4 17.5 %reduce-scatter.45.cloned.1.call-done = bf16[192,1536]{1,0:T(8,128)(2,1)} async-done(((bf16[768,1536]{1,0:T(8,128)(2,1)}), bf16[192,1536]{1,0:T(8,128)(2,1)}) %reduce-scatter.45.cloned.1.call-update) | async-done | bytes 589840
  706.1 22.0 %reduce-scatter.23.cloned.1.call-done = bf16[192,384]{1,0:T(8,128)(2,1)} async-done(((bf16[768,384]{1,0:T(8,128)(2,1)}), bf16[192,384]{1,0:T(8,128)(2,1)}) %reduce-scatter.23.cloned.1.call-update) | async-done | bytes 147472 | tf_op jit(solution)/shard_map/reduce_scatter | solution.py:489
  728.0 22.5 %reduce-scatter.25.cloned.1.call-done = bf16[192,384]{1,0:T(8,128)(2,1)} async-done(((bf16[768,384]{1,0:T(8,128)(2,1)}), bf16[192,384]{1,0:T(8,128)(2,1)}) %reduce-scatter.25.cloned.1.call-update) | async-done | bytes 147472 | tf_op jit(solution)/shard_map/reduce_scatter | solution.py:489
  750.6 22.7 %reduce-scatter.27.cloned.1.call-done = bf16[192,384]{1,0:T(8,128)(2,1)} async-done(((bf16[768,384]{1,0:T(8,128)(2,1)}), bf16[192,384]{1,0:T(8,128)(2,1)}) %reduce-scatter.27.cloned.1.call-update) | async-done | bytes 147472 | tf_op jit(solution)/shard_map/reduce_scatter | solution.py:489
  773.2 48.7 %reduce-scatter.33.cloned.1.call-done = bf16[192,1536]{1,0:T(8,128)(2,1)} async-done(((bf16[768,1536]{1,0:T(8,128)(2,1)}), bf16[192,1536]{1,0:T(8,128)(2,1)}) %reduce-scatter.33.cloned.1.call-update) | async-done | bytes 589840 | tf_op jit(solution)/shard_map/reduce_scatter | solution.py:489
  827.7 41.5 %all-reduce = (f32[768]{0:T(1024)S(1)}, f32[768]{0:T(1024)S(1)}, f32[768]{0:T(1024)}, f32[768]{0:T(1024)}, f32[768]{0:T(1024)}, /*index=5*/f32[3072]{0:T(1024)S(...) all-reduce(f32[768]{0:T(1024)S(1)} %dynamic_update_slice.16, ...), channel_id=1, replica_groups=mesh['dp'=4,'context'=4,'tensor'=2] {'dp','context','tensor'}, use_global_device_ids=true, to_apply=%region_12.13 | all-reduce | flops 9222 | bytes 73776 | tf_op jit(solution)/shard_map/psum | solution.py:521
  872.9 43.2 %all-gather.32.cloned.1.call-done = bf16[4,512,768]{2,1,0:T(8,128)(2,1)} async-done(((bf16[2,512,768]{2,1,0:T(8,128)(2,1)}), bf16[4,512,768]{2,1,0:T(8,128)(2,1)}) %all-gather.32.cloned.1.call-update) | async-done | bytes 3145744 | tf_op jit(solution)/shard_map/all_gather | solution.py:380
  921.3 50.0 %all-reduce.4.cloned.1.call-done = (bf16[384,192]{1,0:T(8,128)(2,1)}, bf16[1536,192]{1,0:T(8,128)(2,1)}, bf16[192,384]{1,0:T(8,128)(2,1)}, bf16[192,384]{1,0:T(8...) async-done(((bf16[384,192]{1,0:T(8,128)(2,1)}, bf16[1536,192]{1,0:T(8,128)(2,1)}, bf16[192,384]{1,0:T(8,128)(2,1)}, bf16[192,384]{1,0:T(8,128)(2,1)}, ...) | async-done | bytes 1769488 | tf_op jit(solution)/shard_map/psum | solution.py:490
  (306 shorter events, 225.1 us)
Async XLA Ops:
  7.2 89.2 %all-gather.22.cloned.1.call-start = ((), (), s32[]{:S(2)}) async-start(), calls=%async_computation.16 | async-start | bytes 2949120 | tf_op jit(solution)/shard_map/all_gather | solution.py:387
  8.0 111.2 %all-gather.18.cloned.1.call-start = ((), (), s32[]{:S(2)}) async-start(), calls=%async_computation.14 | async-start | bytes 1769472 | tf_op jit(solution)/shard_map/all_gather | solution.py:386
  29.8 104.8 %all-gather.16.cloned.1.call-start = ((), (), s32[]{:S(2)}) async-start(), calls=%async_computation.13 | async-start | bytes 1769472 | tf_op jit(solution)/shard_map/all_gather | solution.py:386
  54.7 104.1 %all-gather.14.cloned.1.call-start = ((), (), s32[]{:S(2)}) async-start(), calls=%async_computation.12 | async-start | bytes 1769472 | tf_op jit(solution)/shard_map/all_gather | solution.py:386
  78.7 135.9 %all-gather.26.cloned.1.call-start = ((), (), s32[]{:S(2)}) async-start(), calls=%async_computation.18 | async-start | bytes 2949120 | tf_op jit(solution)/shard_map/all_gather | solution.py:387
  79.3 154.6 %all-gather.20.cloned.1.call-start = ((), (), s32[]{:S(2)}) async-start(), calls=%async_computation.15 | async-start | bytes 1769472 | tf_op jit(solution)/shard_map/all_gather | solution.py:386
  96.4 201.8 %all-gather.24.cloned.1.call-start = ((), (), s32[]{:S(2)}) async-start(), calls=%async_computation.17 | async-start | bytes 7077888 | tf_op jit(solution)/shard_map/all_gather | solution.py:386
  97.1 265.3 %all-gather.28.cloned.1.call-start = ((), (), s32[]{:S(2)}) async-start(), calls=%async_computation.19 | async-start | bytes 7077888 | tf_op jit(solution)/shard_map/all_gather | solution.py:386
  214.7 301.3 %reduce-scatter.29.cloned.1.call-start = ((), (), s32[]{:S(2)}) async-start(), calls=%async_computation.25 | async-start | bytes 1769472 | tf_op jit(solution)/shard_map/reduce_scatter | solution.py:488
  218.6 153.3 %collective-permute-start.4 = (bf16[512,768]{0,1:T(8,128)(2,1)}, bf16[512,768]{0,1:T(8,128)(2,1)S(1)}, u32[]{:S(2)}, u32[]{:S(2)}) collective-permute-start(bf16[512,768]{0,1:T(8,128)(2,1)} %bitcast.17), channel_id=1, source_target_pairs={{0,4},{2,6},{4,0},{6,2},{1,5},{3,7},{5,1},{7,3},{8,12},{10,14},{12... | collective-permute-start | bytes 2359304 | tf_op jit(solution)/shard_map/ppermute | solution.py:347
  411.5 106.7 %reduce-scatter.35.cloned.1.call-start = ((), (), s32[]{:S(2)}) async-start(), calls=%async_computation.28 | async-start | bytes 7077888 | tf_op jit(solution)/shard_map/reduce_scatter | solution.py:488
  420.7 102.0 %reduce-scatter.37.cloned.1.call-start = ((), (), s32[]{:S(2)}) async-start(), calls=%async_computation.29 | async-start | bytes 1769472
  494.9 48.8 %reduce-scatter.39.cloned.1.call-start = ((), (), s32[]{:S(2)}) async-start(), calls=%async_computation.30 | async-start | bytes 1769472
  500.4 67.4 %reduce-scatter.41.cloned.1.call-start = ((), (), s32[]{:S(2)}) async-start(), calls=%async_computation.31 | async-start | bytes 1769472
  506.0 124.1 %reduce-scatter.31.cloned.1.call-start = ((), (), s32[]{:S(2)}) async-start(), calls=%async_computation.26 | async-start | bytes 7077888 | tf_op jit(solution)/shard_map/reduce_scatter | solution.py:488
  515.9 168.6 %reduce-scatter.43.cloned.1.call-start = ((), (), s32[]{:S(2)}) async-start(), calls=%async_computation.32 | async-start | bytes 737280
  518.1 185.8 %reduce-scatter.45.cloned.1.call-start = ((), (), s32[]{:S(2)}) async-start(), calls=%async_computation.33 | async-start | bytes 2949120
  522.5 205.6 %reduce-scatter.23.cloned.1.call-start = ((), (), s32[]{:S(2)}) async-start(), calls=%async_computation.22 | async-start | bytes 737280 | tf_op jit(solution)/shard_map/reduce_scatter | solution.py:489
  524.9 225.7 %reduce-scatter.25.cloned.1.call-start = ((), (), s32[]{:S(2)}) async-start(), calls=%async_computation.23 | async-start | bytes 737280 | tf_op jit(solution)/shard_map/reduce_scatter | solution.py:489
  545.9 227.3 %reduce-scatter.27.cloned.1.call-start = ((), (), s32[]{:S(2)}) async-start(), calls=%async_computation.24 | async-start | bytes 737280 | tf_op jit(solution)/shard_map/reduce_scatter | solution.py:489
  569.9 252.0 %reduce-scatter.33.cloned.1.call-start = ((), (), s32[]{:S(2)}) async-start(), calls=%async_computation.27 | async-start | bytes 2949120 | tf_op jit(solution)/shard_map/reduce_scatter | solution.py:489
  630.1 242.9 %all-gather.30.cloned.1.call-start = ((), (), s32[]{:S(2)}) async-start(), calls=%async_computation.20 | async-start | bytes 4718592 | tf_op jit(solution)/shard_map/all_gather | solution.py:380
  660.1 256.1 %all-gather.32.cloned.1.call-start = ((), (), s32[]{:S(2)}) async-start(), calls=%async_computation.21 | async-start | bytes 4718592 | tf_op jit(solution)/shard_map/all_gather | solution.py:380
  684.4 286.9 %all-reduce.4.cloned.1.call-start = ((), (), s32[]{:S(2)}) async-start(), calls=%async_computation.34 | async-start | bytes 4030464 | tf_op jit(solution)/shard_map/psum | solution.py:490
  (55 other events, 1797.3 us)
Sparse Core Ops, SparseCore 0:
  9.6 76.6 all-gather.21
  87.9 22.2 all-gather.17
  111.8 22.7 all-gather.15
  136.0 22.7 all-gather.13
  160.2 50.4 all-gather.25
  212.2 21.6 all-gather.19
  235.5 62.6 all-gather.23
  299.7 62.6 all-gather.27
  411.6 21.7 reduce-scatter.28
  435.7 59.9 reduce-scatter.34
  498.0 21.7 reduce-scatter.36
  521.9 21.7 reduce-scatter.38
  545.9 21.7 reduce-scatter.40
  570.0 59.9 reduce-scatter.30
  632.7 21.9 reduce-scatter.42
  657.4 46.4 reduce-scatter.44
  706.6 21.4 reduce-scatter.22
  730.2 20.3 reduce-scatter.24
  752.8 20.3 reduce-scatter.26
  775.4 46.4 reduce-scatter.32
  823.4 45.8 all-gather.29
  871.4 44.6 all-gather.31
  920.1 51.1 all-reduce.3

commit v2 on v1

--- a/solution.py
+++ b/solution.py
@@ -260,7 +260,7 @@
         scratch_shapes=[pltpu.VMEM((width // PAIR, PAIR, PAIR), jnp.float32)],
         compiler_params=ROOM,
         cost_estimate=pl.CostEstimate(
-            flops=length * width * 1024 * 6, bytes_accessed=length * width * 8,
+            flops=length * width * 1024 * 60, bytes_accessed=length * width * 8,
             transcendentals=length * width * 8,
         ),
         name="attend",
@@ -282,11 +282,590 @@
         ],
         compiler_params=ROOM,
         cost_estimate=pl.CostEstimate(
-            flops=length * width * 1024 * 15, bytes_accessed=length * width * 14,
+            flops=length * width * 1024 * 70, bytes_accessed=length * width * 14,
             transcendentals=length * width * 8,
         ),
         name="attend_back",
     )(table, wide, q, k, v, do, key_code, query_code, lse)
+
+
+GROUPS = 8
+DUOS = GROUPS // 2
+TILE = 256
+ANY_SPEC = pl.BlockSpec(memory_space=pl.ANY)
+DMA = pltpu.SemaphoreType.DMA
+WIDE_ROOM = pltpu.CompilerParams(vmem_limit_bytes=63 * 1024 * 1024)
+
+
+def normalize(values):
+    row_mean = jnp.mean(values, -1, keepdims=True)
+    centered = values - row_mean
+    row_var = jnp.mean(centered * centered, -1, keepdims=True)
+    inverse = lax.rsqrt(row_var + EPSILON)
+    return centered * inverse, inverse
+
+
+def normalize_back(grad, unit, inverse):
+    return inverse * (
+        grad
+        - jnp.mean(grad, -1, keepdims=True)
+        - unit * jnp.mean(grad * unit, -1, keepdims=True)
+    )
+
+
+def gelu_both(u):
+    root = 0.7978845608028654
+    square = u * u
+    inner = jnp.tanh(u * (root + (root * 0.044715) * square))
+    half = 0.5 + 0.5 * inner
+    slope = half + u * (0.5 - 0.5 * (inner * inner)) * (root + (3.0 * root * 0.044715) * square)
+    return u * half, slope
+
+
+def start_copies(pairs, sem):
+    copies = [pltpu.make_async_copy(src, dst, sem.at[i]) for i, (src, dst) in enumerate(pairs)]
+    for copy in copies:
+        copy.start()
+    return copies
+
+
+def wait_copies(copies):
+    for copy in copies:
+        copy.wait()
+
+
+def my_spot():
+    place = lax.axis_index("context")
+    return lax.axis_index("tensor"), place // 2, place % 2
+
+
+def group_homes():
+    half, turn, share = my_spot()
+    return [
+        ((half + h) % 2, ((turn + t) % 2) * 2 + (share + s) % 2)
+        for s in range(2)
+        for h in range(2)
+        for t in range(2)
+    ]
+
+
+def lanes_of(g, cols):
+    return pl.ds((g % 2) * cols, cols)
+
+
+def project_attend_kernel(
+    table, wide, x0, x1, x2, x3, n0, n1, n2, n3, f0, f1, b_qkv, key_code, query_code,
+    own_ref, other_ref, q_home, k_home, v_home, w_home, lse_ref,
+    x_v, q_v, k_v, v_v, o_v, w_v, acc, in_sem, out_sem, w_sem,
+):
+    span = x0.shape[0]
+    length, width = q_v.shape
+    half, turn, share = my_spot()
+    weights = []
+    for t in range(2):
+        at = (turn + t) % 2
+        homes = [w_v.at[:, at, share], w_v.at[:, at, (share + 1) % 2]]
+        same, swap = ((n0, n2), (n1, n3))[t]
+        copies = [pltpu.make_async_copy(src, homes[0], w_sem.at[t]) for src in (same, swap)]
+
+        @pl.when(half == share)
+        def _():
+            copies[0].start()
+
+        @pl.when(half != share)
+        def _():
+            copies[1].start()
+
+        far = pltpu.make_async_copy((f0, f1)[t], homes[1], w_sem.at[2 + t])
+        far.start()
+        weights += [copies[0], far]
+    loads = start_copies(
+        [(x, x_v.at[pl.ds(i * span, span)]) for i, x in enumerate((x0, x1, x2, x3))], in_sem
+    )
+    wait_copies(weights)
+    w_qkv = w_v[...].reshape(x_v.shape[1], 3 * width)
+    for i in range(4):
+        loads[i].wait()
+        at = pl.ds(i * span, span)
+        value = (dot_nn(x_v[at, :], w_qkv) + b_qkv[...]).astype(jnp.bfloat16)
+        q_v[at, :] = value[:, :width]
+        k_v[at, :] = value[:, width : 2 * width]
+        v_v[at, :] = value[:, 2 * width :]
+    stores = start_copies([(q_v, q_home), (k_v, k_home), (v_v, v_home), (w_v, w_home)], out_sem)
+    attend_kernel(table, wide, q_v, k_v, v_v, key_code, query_code, o_v, lse_ref, acc)
+    own_ref[...] = o_v[: length // 2, :]
+    other_ref[...] = o_v[length // 2 :, :]
+    wait_copies(stores)
+
+
+def project_attend(table, wide, chunks, near, far, b_qkv, key_code, query_code):
+    span, features = chunks[0].shape
+    length = 4 * span
+    depth, slim, cols = near[0].shape
+    width = cols // 3
+    bf16, shape = jnp.bfloat16, jax.ShapeDtypeStruct
+    outs = pl.pallas_call(
+        project_attend_kernel,
+        out_shape=(shape((length // 2, width), bf16),) * 2
+        + (shape((length, width), bf16),) * 3
+        + (
+            shape((depth, 2, 2, slim, cols), bf16),
+            shape((length // BLK, 8, PAIR), jnp.float32),
+        ),
+        in_specs=[SMEM_SPEC] * 2 + [ANY_SPEC] * 10 + [VMEM_SPEC] * 3,
+        out_specs=(VMEM_SPEC,) * 2 + (ANY_SPEC,) * 4 + (VMEM_SPEC,),
+        scratch_shapes=[pltpu.VMEM((length, features), bf16)]
+        + [pltpu.VMEM((length, width), bf16)] * 4
+        + [
+            pltpu.VMEM((depth, 2, 2, slim, cols), bf16),
+            pltpu.VMEM((width // PAIR, PAIR, PAIR), jnp.float32),
+            DMA((4,)), DMA((4,)), DMA((4,)),
+        ],
+        compiler_params=WIDE_ROOM,
+        cost_estimate=pl.CostEstimate(
+            flops=length * width * 1024 * 65, bytes_accessed=length * width * 16,
+            transcendentals=length * width * 8,
+        ),
+        name="project_attend",
+    )(table, wide, *chunks, *near, *far, b_qkv, key_code, query_code)
+    att0, att1, q, k, v, w_qkv, lse = outs
+    return att0, att1, q, k, v, lse, w_qkv.reshape(features, cols)
+
+
+def attend_project_kernel(
+    table, wide, x0, x1, x2, x3, do0, do1, q_in, k_in, v_in, w_qkv, key_code, query_code, lse_ref,
+    back_own, back_other, keep_home, send_home, sums,
+    x_v, q_v, k_v, v_v, do_v, d_v, dk_sum, dv_sum, acc, grad_v, in_sem, x_sem, out_sem,
+):
+    f32, bf16 = jnp.float32, jnp.bfloat16
+    span = x0.shape[0]
+    length, width = q_v.shape
+    depth, turns, shares, slim, cols = grad_v.shape
+    half_length = length // 2
+    loads = start_copies(
+        [
+            (q_in, q_v), (k_in, k_v), (v_in, v_v),
+            (do0, do_v.at[pl.ds(0, half_length)]),
+            (do1, do_v.at[pl.ds(half_length, half_length)]),
+        ],
+        in_sem,
+    )
+    x_loads = start_copies(
+        [(x, x_v.at[pl.ds(i * span, span)]) for i, x in enumerate((x0, x1, x2, x3))], x_sem
+    )
+    wait_copies(loads)
+    parts = [d_v.at[:, pl.ds(i * width, width)] for i in range(3)]
+    attend_back_kernel(
+        table, wide, q_v, k_v, v_v, do_v, key_code, query_code, lse_ref,
+        *parts, dk_sum, dv_sum, acc,
+    )
+    wait_copies(x_loads)
+    sums[0:1, :] = jnp.sum(d_v[:, :width].astype(f32), 0, keepdims=True)
+    sums[1:2, :] = jnp.sum(d_v[:, 2 * width :].astype(f32), 0, keepdims=True)
+    grad_v[...] = dot_tn(x_v[...], d_v[...]).astype(bf16).reshape(grad_v.shape)
+    half, turn, share = my_spot()
+    stores = start_copies(
+        [
+            (grad_v.at[:, (turn + t) % 2, who], home.at[t])
+            for t in range(turns)
+            for who, home in ((share, keep_home), ((share + 1) % 2, send_home))
+        ],
+        out_sem,
+    )
+    for i in range(4):
+        value = dot_nt(d_v[pl.ds(i * span, span), :], w_qkv[...])
+        if i < 2:
+            back_own[pl.ds(i * span, span), :] = value
+        else:
+            back_other[pl.ds((i - 2) * span, span), :] = value.astype(bf16)
+    wait_copies(stores)
+
+
+def attend_project(
+    table, wide, chunks, do0, do1, q, k, v, w_qkv, key_code, query_code, lse, depth
+):
+    span, features = chunks[0].shape
+    length, width = q.shape
+    f32, bf16, shape = jnp.float32, jnp.bfloat16, jax.ShapeDtypeStruct
+    slim = features // depth // 4
+    grads = shape((2, depth, slim, 3 * width), bf16)
+    return pl.pallas_call(
+        attend_project_kernel,
+        out_shape=(
+            shape((length // 2, features), f32), shape((length // 2, features), bf16),
+            grads, grads, shape((8, width), f32),
+        ),
+        in_specs=[SMEM_SPEC] * 2 + [ANY_SPEC] * 9 + [VMEM_SPEC] * 4,
+        out_specs=(VMEM_SPEC,) * 2 + (ANY_SPEC,) * 2 + (VMEM_SPEC,),
+        scratch_shapes=[pltpu.VMEM((length, features), bf16)]
+        + [pltpu.VMEM((length, width), bf16)] * 4
+        + [pltpu.VMEM((length, 3 * width), bf16)]
+        + [pltpu.VMEM((length, width), f32)] * 2
+        + [
+            pltpu.VMEM((width // PAIR, PAIR, PAIR), f32),
+            pltpu.VMEM((depth, 2, 2, slim, 3 * width), bf16),
+            DMA((5,)), DMA((4,)), DMA((4,)),
+        ],
+        compiler_params=WIDE_ROOM,
+        cost_estimate=pl.CostEstimate(
+            flops=length * width * 1024 * 85, bytes_accessed=length * width * 30,
+            transcendentals=length * width * 8,
+        ),
+        name="attend_project",
+    )(table, wide, *chunks, do0, do1, q, k, v, w_qkv, key_code, query_code, lse)
+
+
+def load_weights(groups, w_up, w_dn, w_out, up_sem, dn_sem, wo_sem):
+    depth, deep, cols = groups[0].shape
+    thin = w_up.shape[2]
+    slim = deep - 2 * thin
+    homes = group_homes()
+    out_loads = []
+    for g in range(GROUPS):
+        half, at = homes[g]
+        for d in range(depth):
+            spot = pl.ds(pl.multiple_of(d * thin + at * slim, 16), slim)
+            out_loads.append(
+                pltpu.make_async_copy(
+                    groups[g].at[d, pl.ds(2 * thin, slim)], w_out.at[half, spot], wo_sem.at[g, d]
+                )
+            )
+    up_loads = [
+        pltpu.make_async_copy(
+            groups[g].at[:, pl.ds(0, thin)], w_up.at[g // 2, :, :, lanes_of(g, cols)], up_sem.at[g]
+        )
+        for g in range(GROUPS)
+    ]
+    dn_loads = [
+        pltpu.make_async_copy(
+            groups[g].at[:, pl.ds(thin, thin)],
+            w_dn.at[g // 2, :, :, lanes_of(g, cols)],
+            dn_sem.at[g],
+        )
+        for g in range(GROUPS)
+    ]
+    return out_loads, up_loads, dn_loads
+
+
+def whole(ref, g):
+    depth, thin, cols = ref.shape[1:]
+    return ref[g].reshape(depth * thin, cols)
+
+
+def ffn_front_kernel(att0, att1, x0, x1, g0, g1, *rest):
+    groups = rest[:GROUPS]
+    (
+        valid, vectors, b_up,
+        out0_home, out1_home, slope_home, g_second_home, unit_home, norm_t_home, near_ref, far_ref,
+        inverse_ref, sums,
+        att_v, x_v, g_v, w_up, w_dn, w_out, act, slope, normed_low,
+        out_v, g_second_v, unit_v, norm_t, g_ffn_t, stage,
+        in_sem, up_sem, dn_sem, wo_sem, stage_sem, home_sem, end_sem,
+    ) = rest[GROUPS:]
+    f32, bf16 = jnp.float32, jnp.bfloat16
+    rows, width = x_v.shape
+    span = x0.shape[0]
+    depth, deep, cols = groups[0].shape
+    half, turn, share = my_spot()
+    other = (share + 1) % 2
+    out_loads, up_loads, dn_loads = load_weights(groups, w_up, w_dn, w_out, up_sem, dn_sem, wo_sem)
+    loads = start_copies(
+        [(a, att_v.at[:, lanes_of(i, cols)]) for i, a in enumerate((att0, att1))]
+        + [(x, x_v.at[pl.ds(i * span, span)]) for i, x in enumerate((x0, x1))]
+        + [(g, g_v.at[pl.ds(i * span, span)]) for i, g in enumerate((g0, g1))],
+        in_sem,
+    )
+    for copy in out_loads + up_loads + dn_loads:
+        copy.start()
+    sums[...] = jnp.zeros_like(sums)
+    wait_copies(loads + out_loads)
+    b_out, gain1, shift1, b_down, gain2, shift2 = (vectors[i : i + 1, :] for i in range(6))
+
+    def add_sum(index, value):
+        sums[index : index + 1, :] += jnp.sum(value, 0, keepdims=True)
+
+    def homes(tile):
+        at = pl.ds(pl.multiple_of(tile * TILE, TILE), TILE)
+        return [
+            pltpu.make_async_copy(src, dst, home_sem.at[i, tile])
+            for i, (src, dst) in enumerate(
+                [
+                    (slope.at[:, at], slope_home.at[:, at]),
+                    (g_second_v.at[at], g_second_home.at[at]),
+                    (unit_v.at[at], unit_home.at[at]),
+                ]
+            )
+        ]
+
+    def tile_step(tile, carry):
+        at = pl.ds(pl.multiple_of(tile * TILE, TILE), TILE)
+        live = valid[at, :]
+        attn = b_out + dot_nt(att_v[at, :], jnp.concatenate([w_out[share], w_out[other]], 1))
+        x = x_v[at, :].astype(f32)
+        first = x + attn
+        add_sum(6, live * (x * x))
+        add_sum(7, live * (first * first))
+        add_sum(9, live * (attn * attn))
+        unit1, inverse1 = normalize(first)
+        unit_v[at, :] = unit1
+        inverse_ref[at, :] = inverse1
+        normed = unit1 * gain1 + shift1
+        low = normed.astype(bf16)
+        normed_low[...] = low
+        norm_t[:, at] = low.T
+
+        @pl.when(tile == 0)
+        def _():
+            wait_copies(up_loads + dn_loads)
+
+        def up_step(g, ffn):
+            pre = dot_nn(normed_low[...], whole(w_up, g)) + b_up[pl.ds(g, 1), :]
+            value, rise = gelu_both(pre)
+            value = value.astype(bf16)
+            act[g, at, :] = value
+            slope[g, at, :] = rise.astype(bf16)
+            return ffn + dot_nt(value, whole(w_dn, g))
+
+        ffn = lax.fori_loop(0, DUOS, up_step, jnp.broadcast_to(b_down, (TILE, width)))
+        second = normed + ffn
+        add_sum(8, live * (second * second))
+        add_sum(10, live * (ffn * ffn))
+        unit2, inverse2 = normalize(second)
+        out_v[at, :] = (unit2 * gain2 + shift2).astype(bf16)
+        g_out = g_v[at, :].astype(f32)
+        add_sum(4, g_out * unit2)
+        add_sum(5, g_out)
+        g_second = normalize_back(g_out * gain2, unit2, inverse2)
+        g_second_v[at, :] = g_second
+        g_ffn = g_second.astype(bf16)
+        add_sum(3, g_ffn.astype(f32))
+        g_ffn_t[:, at] = g_ffn.T
+        for copy in homes(tile):
+            copy.start()
+        return carry
+
+    lax.fori_loop(0, rows // TILE, tile_step, 0)
+    last = start_copies(
+        [
+            (norm_t, norm_t_home),
+            (out_v.at[pl.ds(0, span)], out0_home),
+            (out_v.at[pl.ds(span, span)], out1_home),
+        ],
+        end_sem,
+    )
+    stores = [None] * GROUPS
+    for duo in range(DUOS):
+        down = dot_nn(g_ffn_t[...], act[duo]).astype(bf16).reshape(depth, -1, 2 * cols)
+        for g in (2 * duo, 2 * duo + 1):
+            slot = g % 4
+            if g >= 4:
+                stores[g - 4].wait()
+            stage[slot] = down[:, :, (g % 2) * cols : (g % 2 + 1) * cols]
+            home = near_ref.at[g] if g < DUOS else far_ref.at[g - DUOS]
+            stores[g] = pltpu.make_async_copy(stage.at[slot], home, stage_sem.at[slot])
+            stores[g].start()
+    for tile in range(rows // TILE):
+        wait_copies(homes(tile))
+    wait_copies(stores[-4:] + last)
+
+
+def ffn_front(att0, att1, x_chunks, g_chunks, groups, valid, vectors, b_up):
+    rows, part = att0.shape
+    width = x_chunks[0].shape[1]
+    depth, deep, cols = groups[0].shape
+    thin = width // depth
+    f32, bf16, shape = jnp.float32, jnp.bfloat16, jax.ShapeDtypeStruct
+    grads = shape((DUOS, depth, thin, cols), bf16)
+    weights = pltpu.VMEM((DUOS, depth, thin, 2 * cols), bf16)
+    flat = pltpu.VMEM((rows, width), bf16)
+    tall = pltpu.VMEM((rows, width), f32)
+    deep_rows = pltpu.VMEM((DUOS, rows, 2 * cols), bf16)
+    turned = pltpu.VMEM((width, rows), bf16)
+    return pl.pallas_call(
+        ffn_front_kernel,
+        out_shape=(
+            shape((rows // 2, width), bf16), shape((rows // 2, width), bf16),
+            shape((DUOS, rows, 2 * cols), bf16),
+            shape((rows, width), f32), shape((rows, width), f32), shape((width, rows), bf16),
+            grads, grads, shape((rows, 1), f32), shape((16, width), f32),
+        ),
+        in_specs=[ANY_SPEC] * (6 + GROUPS) + [VMEM_SPEC] * 3,
+        out_specs=(ANY_SPEC,) * 8 + (VMEM_SPEC,) * 2,
+        scratch_shapes=[
+            flat, flat, flat, weights, weights, pltpu.VMEM((2, width, part), bf16),
+            deep_rows, deep_rows, pltpu.VMEM((TILE, width), bf16),
+            flat, tall, tall, turned, turned, pltpu.VMEM((4, depth, thin, cols), bf16),
+            DMA((6,)), DMA((GROUPS,)), DMA((GROUPS,)), DMA((GROUPS, depth)), DMA((4,)),
+            DMA((3, rows // TILE)), DMA((3,)),
+        ],
+        compiler_params=WIDE_ROOM,
+        cost_estimate=pl.CostEstimate(
+            flops=38 * 10**9, bytes_accessed=40 * 10**6, transcendentals=rows * GROUPS * cols
+        ),
+        name="ffn_front",
+    )(att0, att1, *x_chunks, *g_chunks, *groups, valid, vectors, b_up)
+
+
+def ffn_rear_kernel(att0, att1, slope_in, g_second_in, unit_in, norm_t_in, *rest):
+    groups = rest[:GROUPS]
+    (
+        inverse_ref, vectors,
+        g_first_home, g_att0_home, g_att1_home, near_ref, far_ref, sums, up_sums,
+        att_v, slope, g_second_v, unit_v, norm_t, w_up, w_dn, w_out, g_pre,
+        g_first_v, g_att_v, g_attn_t, stage,
+        in_sem, up_sem, dn_sem, wo_sem, stage_sem, home_sem,
+    ) = rest[GROUPS:]
+    f32, bf16 = jnp.float32, jnp.bfloat16
+    rows, width = unit_v.shape
+    depth, deep, cols = groups[0].shape
+    thin = w_up.shape[2]
+    slim = deep - 2 * thin
+    half, turn, share = my_spot()
+    other = (share + 1) % 2
+    out_loads, up_loads, dn_loads = load_weights(groups, w_up, w_dn, w_out, up_sem, dn_sem, wo_sem)
+    wait_order = [
+        pltpu.make_async_copy(src, dst, in_sem.at[i])
+        for i, (src, dst) in enumerate(
+            [
+                (g_second_in, g_second_v), (slope_in, slope), (unit_in, unit_v),
+                (norm_t_in, norm_t), (att0, att_v.at[:, lanes_of(0, cols)]),
+                (att1, att_v.at[:, lanes_of(1, cols)]),
+            ]
+        )
+    ]
+    for copy in wait_order[:1] + dn_loads + wait_order[1:2] + up_loads + wait_order[2:3]:
+        copy.start()
+    for copy in out_loads + wait_order[3:]:
+        copy.start()
+    sums[...] = jnp.zeros_like(sums)
+    up_sums[...] = jnp.zeros_like(up_sums)
+    gain1 = vectors[1:2, :]
+    wait_copies(wait_order[:1] + dn_loads + wait_order[1:2])
+    out_weight = lambda: jnp.concatenate([w_out[share], w_out[other]], 1)
+
+    def add_sum(index, value):
+        sums[index : index + 1, :] += jnp.sum(value, 0, keepdims=True)
+
+    def tile_step(tile, carry):
+        at = pl.ds(pl.multiple_of(tile * TILE, TILE), TILE)
+
+        @pl.when(tile == 0)
+        def _():
+            wait_copies(up_loads + wait_order[2:] + out_loads)
+
+        g_second = g_second_v[at, :]
+        g_ffn = g_second.astype(bf16)
+
+        def back_step(g, total):
+            grad = (dot_nn(g_ffn, whole(w_dn, g)) * slope[g, at, :].astype(f32)).astype(bf16)
+            g_pre[g, at, :] = grad
+            up_sums[pl.ds(g, 1), :] += jnp.sum(grad.astype(f32), 0, keepdims=True)
+            return total + dot_nt(grad, whole(w_up, g))
+
+        g_normed = lax.fori_loop(0, DUOS, back_step, g_second)
+        unit1 = unit_v[at, :]
+        add_sum(1, g_normed * unit1)
+        add_sum(2, g_normed)
+        g_first = normalize_back(g_normed * gain1, unit1, inverse_ref[at, :])
+        g_first_v[at, :] = g_first
+        g_attn = g_first.astype(bf16)
+        add_sum(0, g_attn.astype(f32))
+        g_attn_t[:, at] = g_attn.T
+        g_att_v[at, :] = dot_nn(g_attn, out_weight()).astype(bf16)
+        return carry
+
+    lax.fori_loop(0, rows // TILE, tile_step, 0)
+    homes = start_copies(
+        [
+            (g_att_v.at[:, lanes_of(0, cols)], g_att0_home),
+            (g_att_v.at[:, lanes_of(1, cols)], g_att1_home),
+            (g_first_v, g_first_home),
+        ],
+        home_sem,
+    )
+    both = dot_nn(g_attn_t[...], att_v[...]).astype(bf16)
+    w_out[share] = both[:, :cols]
+    w_out[other] = both[:, cols:]
+    spots = group_homes()
+    stores = [None] * GROUPS
+    for duo in range(DUOS):
+        up = dot_nn(norm_t[...], g_pre[duo]).astype(bf16).reshape(depth, thin, 2 * cols)
+        for g in (2 * duo, 2 * duo + 1):
+            slot = g % 4
+            if g >= 4:
+                stores[g - 4].wait()
+            stage[slot, :, pl.ds(0, thin), :] = up[:, :, (g % 2) * cols : (g % 2 + 1) * cols]
+            where, at = spots[g]
+            for d in range(depth):
+                spot = pl.ds(pl.multiple_of(d * thin + at * slim, 16), slim)
+                stage[slot, d, pl.ds(thin, slim), :] = w_out[where, spot, :]
+            home = near_ref.at[g] if g < DUOS else far_ref.at[g - DUOS]
+            stores[g] = pltpu.make_async_copy(stage.at[slot], home, stage_sem.at[slot])
+            stores[g].start()
+    wait_copies(stores[-4:] + homes)
+
+
+def ffn_rear(att0, att1, slope, g_second, unit, norm_t, groups, inverse, vectors):
+    rows, part = att0.shape
+    width = unit.shape[1]
+    depth, deep, cols = groups[0].shape
+    thin = width // depth
+    f32, bf16, shape = jnp.float32, jnp.bfloat16, jax.ShapeDtypeStruct
+    grads = shape((DUOS, depth, deep - thin, cols), bf16)
+    weights = pltpu.VMEM((DUOS, depth, thin, 2 * cols), bf16)
+    flat = pltpu.VMEM((rows, width), bf16)
+    tall = pltpu.VMEM((rows, width), f32)
+    deep_rows = pltpu.VMEM((DUOS, rows, 2 * cols), bf16)
+    turned = pltpu.VMEM((width, rows), bf16)
+    return pl.pallas_call(
+        ffn_rear_kernel,
+        out_shape=(
+            shape((rows, width), f32), shape((rows, part), bf16), shape((rows, part), bf16),
+            grads, grads, shape((16, width), f32), shape((DUOS, 2 * cols), f32),
+        ),
+        in_specs=[ANY_SPEC] * (6 + GROUPS) + [VMEM_SPEC] * 2,
+        out_specs=(ANY_SPEC,) * 5 + (VMEM_SPEC,) * 2,
+        scratch_shapes=[
+            flat, deep_rows, tall, tall, turned, weights, weights,
+            pltpu.VMEM((2, width, part), bf16), deep_rows, tall, flat, turned,
+            pltpu.VMEM((4, depth, deep - thin, cols), bf16),
+            DMA((6,)), DMA((GROUPS,)), DMA((GROUPS,)), DMA((GROUPS, depth)), DMA((4,)), DMA((3,)),
+        ],
+        compiler_params=WIDE_ROOM,
+        cost_estimate=pl.CostEstimate(
+            flops=38 * 10**9, bytes_accessed=40 * 10**6, transcendentals=0
+        ),
+        name="ffn_rear",
+    )(att0, att1, slope, g_second, unit, norm_t, *groups, inverse, vectors)
+
+
+def gather_chunks_kernel(c0, c1, c2, c3, home, held, ready, in_sem, out_sem):
+    half, turn, share = my_spot()
+    loads = start_copies([(c, held.at[i]) for i, c in enumerate((c0, c1, c2, c3))], in_sem)
+    stores = []
+    for i in range(4):
+        loads[i].wait()
+        ready[i] = held[i].astype(ready.dtype)
+        at = ((half + i // 2) % 2) * 2 + (turn + i) % 2
+        stores.append(pltpu.make_async_copy(ready.at[i], home.at[at], out_sem.at[i]))
+        stores[i].start()
+    wait_copies(stores)
+
+
+def gather_chunks(chunks, dtype):
+    span, width = chunks[0].shape
+    return pl.pallas_call(
+        gather_chunks_kernel,
+        out_shape=jax.ShapeDtypeStruct((4, span, width), dtype),
+        in_specs=[ANY_SPEC] * 4,
+        out_specs=ANY_SPEC,
+        scratch_shapes=[
+            pltpu.VMEM((4, span, width), chunks[0].dtype), pltpu.VMEM((4, span, width), dtype),
+            DMA((4,)), DMA((4,)),
+        ],
+        compiler_params=WIDE_ROOM,
+        name="gather_chunks",
+    )(*chunks)
 
 
 def layer_norm(values, norm_gain, norm_shift):
@@ -326,45 +905,96 @@
     length = segment_ids.shape[1]
     places = length // span
     halves = lax.axis_size("tensor")
+    depth = lax.axis_size("dp")
     turns = seqs // halves
     shares = places // turns
     my_half = lax.axis_index("tensor")
     my_place = lax.axis_index("context")
+    my_depth = lax.axis_index("dp")
     my_turn, my_share = my_place // shares, my_place % shares
     my_seq = my_half * turns + my_turn
     blocks = length // BLK
     rows = turns * span
-    everyone = ("dp", "context", "tensor")
-
-    def send_turn(value, step):
-        if step % turns == 0:
+    spots = [(h, t) for h in range(halves) for t in range(turns)]
+
+    def send(value, half=0, turn=0, share=0):
+        if half % halves == 0 and turn % turns == 0 and share % shares == 0:
             return value
-        pairs = [
-            (t * shares + s, ((t + step) % turns) * shares + s)
-            for t in range(turns)
-            for s in range(shares)
-        ]
-        return lax.ppermute(value, "context", pairs)
-
-    def send_share(value, step):
-        if step % shares == 0:
-            return value
-        pairs = [
-            (t * shares + s, t * shares + (s + step) % shares)
-            for t in range(turns)
-            for s in range(shares)
-        ]
-        return lax.ppermute(value, "context", pairs)
+        pairs = []
+        for h in range(halves):
+            for t in range(turns):
+                for s in range(shares):
+                    to_place = (t + turn) % turns * shares + (s + share) % shares
+                    pairs.append(
+                        ((t * shares + s) * halves + h, to_place * halves + (h + half) % halves)
+                    )
+        return lax.ppermute(value, ("context", "tensor"), pairs)
+
+    def send_deep(value, step):
+        return lax.ppermute(value, "dp", [(i, (i + step) % depth) for i in range(depth)])
+
+    def pick(value, index, axis=0):
+        return lax.dynamic_index_in_dim(value, index, axis, keepdims=False)
+
+    def own_slice(value, count, which, axis):
+        size = value.shape[axis] // count
+        return lax.dynamic_slice_in_dim(value, which * size, size, axis)
+
+    def gather_deep(value):
+        if depth > 4:
+            return lax.all_gather(value, "dp", axis=0)
+        got = [value] + [send_deep(value, k) for k in range(1, depth)]
+        ring = jnp.stack([got[depth - 1 - i % depth] for i in range(2 * depth - 1)])
+        return lax.dynamic_slice_in_dim(ring, depth - 1 - my_depth, depth, 0)
+
+    def reduce_deep(value):
+        if depth > 4:
+            return lax.psum_scatter(value, "dp", scatter_dimension=0)
+        total = pick(value, my_depth).astype(f32)
+        for k in range(1, depth):
+            total = total + send_deep(pick(value, (my_depth + k) % depth), k).astype(f32)
+        return total.astype(bf16)
+
+    def gather_square(value):
+        near = {spot: send(value, *spot) for spot in spots}
+        near = jnp.stack([near[spot] for spot in spots])
+        return [near] + [send(near, 0, 0, s) for s in range(1, shares)]
+
+    def reduce_square(value):
+        total = value[0].astype(f32)
+        for i, (h, t) in enumerate(spots[1:], 1):
+            total = total + send(value[i], -h, -t).astype(f32)
+        return total.astype(bf16)
+
+    def gather_places(value):
+        near = [send(value, 0, t) for t in range(turns)]
+        near = jnp.stack(near)
+        far = jnp.stack([near] + [send(near, 0, 0, s) for s in range(1, shares)])
+        return jnp.stack(
+            [
+                pick(pick(far, (my_share - s) % shares), (my_turn - t) % turns)
+                for t in range(turns)
+                for s in range(shares)
+            ]
+        )
+
+    def sum_all(value):
+        for step in range(halves.bit_length() - 1):
+            value = value + send(value, 1 << step)
+        size = 1
+        while size < places:
+            value = value + lax.ppermute(value, "context", [(i, i ^ size) for i in range(places)])
+            size *= 2
+        size = 1
+        while size < depth:
+            value = value + lax.ppermute(value, "dp", [(i, i ^ size) for i in range(depth)])
+            size *= 2
+        return value
 
     def bring(value):
         return jnp.concatenate(
             [
-                send_turn(
-                    lax.dynamic_index_in_dim(
-                        value, my_half * turns + (my_turn + k) % turns, 0, keepdims=False
-                    ),
-                    k,
-                )
+                send(pick(value, my_half * turns + (my_turn + k) % turns), 0, k)
                 for k in range(turns)
             ],
             0,
@@ -372,39 +1002,18 @@
 
     def deliver(value):
         value = value.reshape(turns, span, width)
-        got = jnp.stack([send_turn(value[k], -k) for k in range(turns)])
-        order = (jnp.arange(turns) - my_turn) % turns
-        got = jnp.stack(
-            [lax.dynamic_index_in_dim(got, order[t], 0, keepdims=False) for t in range(turns)]
-        )
-        return lax.all_gather(got, "tensor", axis=0, tiled=True)
-
-    def own_slice(value, count, which, axis):
-        size = value.shape[axis] // count
-        return lax.dynamic_slice_in_dim(value, which * size, size, axis)
-
-    both = lambda w, a, b: lax.all_gather(
-        lax.all_gather(w, "dp", axis=a, tiled=True), "tensor", axis=b, tiled=True
-    )
-    w_q, w_k, w_v = (both(w, 0, 1) for w in (query_weight, key_weight, value_weight))
-    w_out = both(output_weight, 1, 0)
-    w_up, w_down = both(up_weight, 0, 1), both(down_weight, 1, 0)
-    b_q, b_v, b_up = (
-        lax.all_gather(b, "tensor", axis=0, tiled=True) for b in (query_bias, value_bias, up_bias)
-    )
-    part = width // shares
-    padded = -(-part // PAIR) * PAIR
-    pad_cols = lambda w: jnp.pad(w, [(0, 0)] * (w.ndim - 1) + [(0, padded - part)])
-    mine = lambda w: pad_cols(own_slice(w, shares, my_share, w.ndim - 1))
-    w_qkv = jnp.concatenate([mine(w_q), mine(w_k), mine(w_v)], 1)
-    b_qkv = jnp.concatenate([mine(b_q), jnp.zeros((padded,), bf16), mine(b_v)]).astype(f32)
-    w_out_mine = jnp.concatenate(
-        [own_slice(w_out, shares, (my_share + k) % shares, 0) for k in range(shares)], 0
-    )
-
-    x_own = bring(hidden_in)
-    g_out = bring(out_grad).astype(f32)
-    x_seq = jnp.concatenate([send_share(x_own, k) for k in range(shares)], 0)
+        got = jnp.stack([send(value[t], h, -t) for h, t in spots])
+        return jnp.stack(
+            [
+                pick(got, (my_half - h) % halves * turns + (t - my_turn) % turns)
+                for h in range(halves)
+                for t in range(turns)
+            ]
+        )
+
+    def after(value, *earlier):
+        return lax.optimization_barrier((value, *earlier))[0]
+
     per = span // BLK
 
     def place(block_ids):
@@ -426,105 +1035,352 @@
             ]
         )
 
-    seg = in_order(lax.dynamic_index_in_dim(segment_ids, my_seq, 0, keepdims=False))
-    live = in_order(lax.dynamic_index_in_dim(token_valid, my_seq, 0, keepdims=False))
-    random_seq = lax.dynamic_index_in_dim(random_blocks, my_seq, 0, keepdims=False)
+    seg = in_order(pick(segment_ids, my_seq))
+    live = in_order(pick(token_valid, my_seq))
+    random_seq = pick(random_blocks, my_seq)
     table, wide = block_tables(random_seq, blocks, place)
     key_code = jnp.broadcast_to(jnp.where(live == 1, seg, -1)[:, None], (length, PAIR))
     query_code = jnp.tile(seg.reshape(blocks, BLK), (1, PAIR // BLK))
-
-    qkv = (jnp.dot(x_seq, w_qkv, preferred_element_type=f32) + b_qkv).astype(bf16)
-    q, k, v = (qkv[:, i * padded : (i + 1) * padded] for i in range(3))
+    half_width = query_weight.shape[1]
+    thin = query_weight.shape[0]
+    slim = thin // places
+    hidden = up_weight.shape[1] // places
+    biases = jnp.concatenate([query_bias, value_bias, up_bias])
+    biases = jnp.stack([send(biases, h) for h in range(halves)])
+    biases = jnp.stack([pick(biases, (my_half - h) % halves) for h in range(halves)])
+    b_q, b_v, b_up = (
+        biases[:, at : at + b.shape[0]].reshape(-1)
+        for b, at in ((query_bias, 0), (value_bias, half_width), (up_bias, 2 * half_width))
+    )
+
+    def spread(value, which, count):
+        return lax.dynamic_update_slice_in_dim(
+            jnp.zeros((value.shape[0] * count,), value.dtype), value, which * value.shape[0], 0
+        )
+
+    def summed(values):
+        flat = sum_all(jnp.concatenate(values))
+        out, at = [], 0
+        for value in values:
+            out.append(flat[at : at + value.shape[0]])
+            at += value.shape[0]
+        return out
+
+    def finish(
+        layer_out, input_grad, qkv_shard, ffn_shard, up_sums, group_at, norm_sums, stats, sum_q, sum_v
+    ):
+        up_natural = jnp.zeros_like(up_sums)
+        for i, at in enumerate(group_at):
+            up_natural = lax.dynamic_update_slice_in_dim(
+                up_natural, up_sums[i * hidden : (i + 1) * hidden], at * hidden, 0
+            )
+        values = [up_natural, *norm_sums, stats]
+        values += [spread(sum_q, my_share, shares), spread(sum_v, my_share, shares)]
+        s_up, s_o, s_g1, s_s1, s_down, s_g2, s_s2, stats, s_q, s_v = summed(values)
+        s_q, s_v, s_up = (own_slice(value, halves, my_half, 0) for value in (s_q, s_v, s_up))
+        input_rms = jnp.sqrt(stats[:5] / (jnp.maximum(stats[5], 1.0) * width))
+        join = lambda w: jnp.moveaxis(w, 0, 1).reshape(thin, -1).astype(f32)
+        shard_up = join(ffn_shard[:, :thin])
+        shard_down = join(ffn_shard[:, thin : 2 * thin]).T
+        shard_o = ffn_shard[:, 2 * thin :].reshape(thin, -1)[:, :half_width].astype(f32).T
+        shard_q, shard_k, shard_v = (qkv_shard[:, i].astype(f32) for i in range(3))
+        return (
+            layer_out, input_grad, shard_q, s_q, shard_k, shard_v, s_v, shard_o, s_o,
+            s_g1, s_s1, shard_up, s_up, shard_down, s_down, s_g2, s_s2, input_rms,
+        )
+
+    if (turns, shares, halves) == (2, 2, 2) and depth <= 4 and rows % TILE == 0:
+        qkv_piece = own_slice(
+            jnp.concatenate([query_weight, key_weight, value_weight], 1), places, my_place, 0
+        )
+        qkv_deep = gather_deep(qkv_piece)
+        x_own = [pick(hidden_in, my_seq)]
+        x_own.append(send(pick(hidden_in, my_half * turns + (my_turn + 1) % turns), 0, 1))
+        near_qkv = [send(qkv_deep, *spot) for spot in spots]
+        mine = my_half == my_share
+        far_qkv = [
+            send(jnp.where(mine, near_qkv[2 + t], near_qkv[t]), 0, 0, 1) for t in range(turns)
+        ]
+        chunks = x_own + [send(x, 0, 0, 1) for x in x_own]
+        own_bias = lambda b: own_slice(b, shares, my_share, 0)
+        b_qkv = jnp.concatenate([own_bias(b_q), jnp.zeros((half_width,), bf16), own_bias(b_v)])
+        b_qkv = b_qkv.astype(f32)[None]
+
+        ffn_piece = jnp.concatenate(
+            [
+                own_slice(up_weight, places, my_place, 1),
+                own_slice(down_weight, places, my_place, 0).T,
+                own_slice(output_weight.T, places, my_place, 0),
+            ],
+            0,
+        )
+        ffn_deep = gather_deep(after(ffn_piece, qkv_deep))
+        g_own = [pick(out_grad, my_seq)]
+        g_next = pick(out_grad, my_half * turns + (my_turn + 1) % turns)
+        g_own.append(send(after(g_next, near_qkv[1]), 0, 1))
+        ffn_deep = after(ffn_deep, *near_qkv[1:])
+        near = [send(ffn_deep, *spot) for spot in spots]
+        group_at = [
+            (
+                (my_half - h) % halves * places
+                + (my_turn - t) % turns * shares
+                + (my_share - s) % shares
+            )
+            for s in range(shares)
+            for h, t in spots
+        ]
+        b_up = jnp.concatenate(
+            [lax.dynamic_slice_in_dim(b_up, at * hidden, hidden) for at in group_at]
+        ).astype(f32)
+
+        att0, att1, q, k, v, lse, w_qkv = project_attend(
+            table, wide, chunks, near_qkv, far_qkv, b_qkv, key_code, query_code
+        )
+        att0, att1, near, g_own = lax.optimization_barrier((att0, att1, near, g_own))
+        att1 = send(att1, 0, 0, 1)
+        groups = near + [send(g, 0, 0, 1) for g in near]
+        vectors = jnp.stack(
+            [output_bias, norm1_gain, norm1_shift, down_bias, norm2_gain, norm2_shift]
+        ).astype(f32)
+        (
+            out0, out1, slope, g_second, unit, norm_t, near_dn, far_dn, inverse, front_sums
+        ) = ffn_front(
+            att0, att1, x_own, g_own, groups, live[:rows, None].astype(f32), vectors,
+            b_up.reshape(DUOS, -1),
+        )
+        out_chunks = [out0, send(out1, 0, 1), send(out0, 1), send(out1, 1, 1)]
+        got_dn = send(far_dn, 0, 0, 1)
+        g_first, g_att0, g_att1, near_uo, far_uo, rear_sums, up_sums = ffn_rear(
+            att0, att1, slope, g_second, unit, norm_t, groups, inverse, vectors
+        )
+        out_chunks, got_dn, g_first, g_att0, g_att1, near_uo, far_uo = lax.optimization_barrier(
+            (out_chunks, got_dn, g_first, g_att0, g_att1, near_uo, far_uo)
+        )
+        got_uo = send(far_uo, 0, 0, 1)
+        g_att1 = send(g_att1, 0, 0, 1)
+        total_dn = (near_dn.astype(f32) + got_dn.astype(f32)).astype(bf16)
+        total_uo = (near_uo.astype(f32) + got_uo.astype(f32)).astype(bf16)
+        parts_dn = [send(total_dn[i], *spots[i]) for i in range(len(spots))]
+        parts_uo = [send(total_uo[i], *spots[i]) for i in range(len(spots))]
+        g_att1 = after(g_att1, total_dn, total_uo)
+        back_own, back_other, keep, swap, head_sums = attend_project(
+            table, wide, chunks, g_att0, g_att1, q, k, v, w_qkv, key_code, query_code, lse, depth
+        )
+        back_own, back_other, keep, swap, parts_dn, parts_uo = lax.optimization_barrier(
+            (back_own, back_other, keep, swap, parts_dn, parts_uo)
+        )
+        back_got = send(back_other, 0, 0, 1)
+        swap = send(swap, 0, 0, 1)
+        pieces = [jnp.where(mine, keep, swap), jnp.where(mine, swap, keep)]
+        square = jnp.stack([pieces[h][t] for h, t in spots])
+        qkv_shard = gather_places(reduce_deep(reduce_square(square)))
+        qkv_shard = qkv_shard.reshape(thin, 3, half_width)
+        total = [
+            sum([p.astype(f32) for p in parts[1:]], parts[0].astype(f32)).astype(bf16)
+            for parts in (parts_dn, parts_uo)
+        ]
+        total = jnp.concatenate([total[1][:, :thin], total[0], total[1][:, thin:]], 1)
+        ffn_shard = gather_places(reduce_deep(total))
+        grads = (g_first + back_own + back_got.astype(f32)).astype(bf16)
+        g0, g1 = grads[:span], grads[span:]
+        grad_chunks = [g0, send(g1, 0, 1), send(g0, 1), send(g1, 1, 1)]
+        norm_sums = [rear_sums[0], rear_sums[1], rear_sums[2]] + [front_sums[i] for i in (3, 4, 5)]
+        stats = jnp.concatenate(
+            [
+                jnp.sum(front_sums[6:11], 1),
+                jnp.sum(live[:rows]).astype(f32)[None],
+                jnp.zeros((2,), f32),
+            ]
+        )
+        return finish(
+            gather_chunks(out_chunks, bf16), gather_chunks(grad_chunks, f32), qkv_shard, ffn_shard,
+            up_sums.reshape(-1), group_at, norm_sums, stats, head_sums[0], head_sums[1],
+        )
+
+    part = width // shares
+    padded = -(-part // PAIR) * PAIR
+    x_own = bring(hidden_in)
+    qkv_piece = own_slice(
+        jnp.concatenate([query_weight, key_weight, value_weight], 1), places, my_place, 0
+    )
+    qkv_all = jnp.stack(gather_square(gather_deep(qkv_piece)))
+    per_half = shares // halves
+    target = my_share // per_half
+    qkv_all = jnp.stack(
+        [
+            pick(
+                pick(qkv_all, (my_share - s) % shares),
+                (my_half - target) % halves * turns + (my_turn - t) % turns,
+            )
+            for t in range(turns)
+            for s in range(shares)
+        ],
+        1,
+    ).reshape(width, 3, half_width)
+    pad_cols = lambda w: jnp.pad(w, [(0, 0)] * (w.ndim - 1) + [(0, padded - part)])
+    mine = lambda w: pad_cols(own_slice(w, per_half, my_share % per_half, w.ndim - 1))
+    w_qkv = mine(qkv_all).reshape(width, 3 * padded)
+    mine_b = lambda b: pad_cols(own_slice(b, shares, my_share, 0))
+    b_qkv = jnp.concatenate([mine_b(b_q), jnp.zeros((padded,), bf16), mine_b(b_v)]).astype(f32)
+
+    ffn_piece = jnp.concatenate(
+        [
+            own_slice(up_weight, places, my_place, 1),
+            own_slice(down_weight, places, my_place, 0).T,
+            jnp.pad(
+                own_slice(output_weight.T, places, my_place, 0),
+                [(0, 0), (0, max(0, hidden - half_width))],
+            ).reshape(-1, hidden),
+        ],
+        0,
+    )
+    ffn_all = gather_square(gather_deep(ffn_piece))
+    groups = [
+        (s, i, ffn_all[s][i]) for s in range(shares) for i in range(len(spots))
+    ]
+    w_up = jnp.concatenate([g[:, :thin].reshape(width, hidden) for _, _, g in groups], 1)
+    w_down_t = jnp.concatenate(
+        [g[:, thin : 2 * thin].reshape(width, hidden) for _, _, g in groups], 1
+    )
+    out_all = jnp.stack(
+        [jnp.stack([g[:, 2 * thin :] for g in ffn_all[s]]) for s in range(shares)]
+    )
+    w_out_t = jnp.stack(
+        [
+            jnp.stack(
+                [
+                    pick(
+                        pick(out_all, (my_share - s) % shares),
+                        (my_half - h) % halves * turns + (my_turn - t) % turns,
+                    )
+                    for t in range(turns)
+                    for s in range(shares)
+                ],
+                1,
+            ).reshape(width, half_width)
+            for h in range(halves)
+        ],
+        1,
+    ).reshape(width, width)
+    w_out_t = jnp.concatenate(
+        [own_slice(w_out_t, shares, (my_share + k) % shares, 1) for k in range(shares)], 1
+    )
+    group_at = [
+        ((my_half - spots[i][0]) % halves * places
+         + (my_turn - spots[i][1]) % turns * shares + (my_share - s) % shares)
+        for s, i, _ in groups
+    ]
+    b_up = jnp.concatenate(
+        [lax.dynamic_slice_in_dim(b_up, at * hidden, hidden) for at in group_at]
+    ).astype(f32)
+
+    g_out = bring(out_grad).astype(f32)
+    x_seq = jnp.concatenate([send(x_own, 0, 0, k) for k in range(shares)], 0)
+    q, k, v = (
+        (
+            jnp.dot(x_seq, w_qkv[:, i * padded : (i + 1) * padded], preferred_element_type=f32)
+            + b_qkv[i * padded : (i + 1) * padded]
+        ).astype(bf16)
+        for i in range(3)
+    )
     att, lse = attend(table, wide, q, k, v, key_code, query_code)
     att = att[:, :part].reshape(shares, rows, part)
-    att_own = jnp.concatenate([send_share(att[s], -s) for s in range(shares)], 1)
-    attn_out = jnp.dot(att_own, w_out_mine, preferred_element_type=f32) + output_bias.astype(f32)
+    att_own = jnp.concatenate([send(att[s], 0, 0, -s) for s in range(shares)], 1)
+    attn_out = lax.dot_general(
+        att_own, w_out_t, (((1,), (1,)), ((), ())), preferred_element_type=f32
+    ) + output_bias.astype(f32)
     x_full = x_own.astype(f32)
     first_sum = x_full + attn_out
     gain_one, shift_one = norm1_gain.astype(f32), norm1_shift.astype(f32)
     normed = layer_norm(first_sum, gain_one, shift_one)
     normed_low = normed.astype(bf16)
-    pre_act = jnp.dot(normed_low, w_up, preferred_element_type=f32) + b_up.astype(f32)
+    pre_act = jnp.dot(normed_low, w_up, preferred_element_type=f32) + b_up
     act_low = gelu_tanh(pre_act).astype(bf16)
-    ffn_out = jnp.dot(act_low, w_down, preferred_element_type=f32) + down_bias.astype(f32)
+    ffn_out = lax.dot_general(
+        act_low, w_down_t, (((1,), (1,)), ((), ())), preferred_element_type=f32
+    ) + down_bias.astype(f32)
     second_sum = normed + ffn_out
     gain_two, shift_two = norm2_gain.astype(f32), norm2_shift.astype(f32)
     layer_out, norm_back = jax.vjp(layer_norm, second_sum, gain_two, shift_two)
     g_second, gain_two_grad, shift_two_grad = norm_back(g_out)
     layer_out = deliver(layer_out.astype(bf16))
     g_ffn = g_second.astype(bf16)
-    g_act = jnp.dot(g_ffn, w_down.T, preferred_element_type=f32)
+    g_act = jnp.dot(g_ffn, w_down_t, preferred_element_type=f32)
     g_pre = jax.vjp(gelu_tanh, pre_act)[1](g_act)[0].astype(bf16)
-    up_part = jnp.dot(normed_low.T, g_pre, preferred_element_type=f32)
-    down_part = jnp.dot(act_low.T, g_ffn, preferred_element_type=f32)
+    up_part = jnp.dot(normed_low.T, g_pre, preferred_element_type=f32).astype(bf16)
+    down_part_t = jnp.dot(g_ffn.T, act_low, preferred_element_type=f32).astype(bf16)
     g_normed = g_second + jnp.dot(g_pre, w_up.T, preferred_element_type=f32)
     g_first, gain_one_grad, shift_one_grad = jax.vjp(layer_norm, first_sum, gain_one, shift_one)[1](
         g_normed
     )
     g_attn = g_first.astype(bf16)
-    out_part = jnp.dot(att_own.T, g_attn, preferred_element_type=f32).astype(bf16)
-    g_att = jnp.dot(g_attn, w_out_mine.T, preferred_element_type=f32).astype(bf16)
+    out_part_t = jnp.dot(g_attn.T, att_own, preferred_element_type=f32).astype(bf16)
+    g_att = jnp.dot(g_attn, w_out_t, preferred_element_type=f32).astype(bf16)
     do = jnp.concatenate(
-        [send_share(own_slice(g_att, shares, s, 1), s) for s in range(shares)], 0
+        [send(own_slice(g_att, shares, s, 1), 0, 0, s) for s in range(shares)], 0
     )
     dq, dk, dv = attend_back(table, wide, q, k, v, pad_cols(do), key_code, query_code, lse)
+
+    out_natural = jnp.concatenate(
+        [own_slice(out_part_t, shares, (s - my_share) % shares, 1) for s in range(shares)], 1
+    ).reshape(depth, turns, shares, slim, halves, half_width)
+
+    def ffn_group(s, i):
+        h, t = spots[i]
+        at = (s * len(spots) + i) * hidden
+        out = pick(out_natural, (my_half - h) % halves, 4)
+        out = pick(pick(out, (my_turn - t) % turns, 1), (my_share - s) % shares, 1)
+        out = jnp.pad(out, [(0, 0), (0, 0), (0, max(0, hidden - half_width))])
+        cut = lambda w: w[:, at : at + hidden].reshape(depth, thin, hidden)
+        return jnp.concatenate(
+            [cut(up_part), cut(down_part_t), out.reshape(depth, -1, hidden)], 1
+        )
+
+    ffn_grads = [
+        jnp.stack([ffn_group(s, i) for i in range(len(spots))]) for s in range(shares)
+    ]
+    total = ffn_grads[0].astype(f32)
+    for s in range(1, shares):
+        total = total + send(ffn_grads[s], 0, 0, -s).astype(f32)
+    ffn_shard = gather_places(reduce_deep(reduce_square(total.astype(bf16))))
     dqkv = jnp.concatenate([dq, dk, dv], 1)
-    qkv_part = jnp.dot(x_seq.T, dqkv, preferred_element_type=f32).astype(bf16)
+    qkv_part = (
+        jnp.dot(x_seq.T, dqkv, preferred_element_type=f32)
+        .astype(bf16)
+        .reshape(depth, turns, shares, slim, 3, padded)[..., :part]
+    )
+    got = jnp.stack(
+        [send(pick(qkv_part, (my_share + s) % shares, 2), 0, 0, s) for s in range(shares)]
+    )
+    got = jnp.stack([pick(got, (my_share - s) % shares) for s in range(shares)], 4)
+    got = got.reshape(depth, turns, slim, 3, halves, half_width)
+    square = jnp.stack(
+        [
+            pick(pick(got, (my_half - h) % halves, 4), (my_turn - t) % turns, 1)
+            for h, t in spots
+        ]
+    ).reshape(len(spots), depth, slim, 3 * half_width)
+    qkv_shard = gather_places(reduce_deep(reduce_square(square))).reshape(thin, 3, half_width)
     back = jnp.dot(dqkv, w_qkv.T, preferred_element_type=f32).reshape(shares, rows, width)
     back_own = back[0]
     for s in range(1, shares):
-        back_own = back_own + send_share(back[s].astype(bf16), -s).astype(f32)
+        back_own = back_own + send(back[s].astype(bf16), 0, 0, -s).astype(f32)
     input_grad = deliver((g_first + back_own).astype(bf16)).astype(f32)
-
-    def spread(value, which, axis):
-        shape = list(value.shape)
-        size = shape[axis]
-        shape[axis] = size * shares
-        return lax.dynamic_update_slice_in_dim(
-            jnp.zeros(shape, value.dtype), value, which * size, axis
-        )
-
-    def shard(value, dp_axis, tensor_axis):
-        value = lax.psum_scatter(value, "tensor", scatter_dimension=tensor_axis, tiled=True)
-        value = lax.psum_scatter(value, "dp", scatter_dimension=dp_axis, tiled=True)
-        return lax.psum(value, "context").astype(f32)
-
-    shard_q, shard_k, shard_v = (
-        shard(spread(qkv_part[:, i * padded : i * padded + part], my_share, 1), 0, 1)
-        for i in range(3)
-    )
-    out_full = jnp.concatenate(
-        [own_slice(out_part, shares, (s - my_share) % shares, 0) for s in range(shares)], 0
-    )
-    shard_o = shard(out_full, 1, 0)
-    shard_up = shard(up_part.astype(bf16), 0, 1)
-    shard_down = shard(down_part.astype(bf16), 1, 0)
 
     sums = lambda value: jnp.sum(value.astype(f32), 0)
     valid = live[:rows].astype(f32)
     squares = lambda member: jnp.sum(valid * jnp.sum(member * member, -1))
     stats = jnp.stack(
-        [squares(m) for m in (x_full, first_sum, second_sum, attn_out, ffn_out)] + [jnp.sum(valid)]
-    )
-    small = [
-        spread(sums(dq)[:part], my_share, 0),
-        spread(sums(dv)[:part], my_share, 0),
-        sums(g_pre),
-        sums(g_attn),
-        gain_one_grad,
-        shift_one_grad,
-        sums(g_ffn),
-        gain_two_grad,
-        shift_two_grad,
-        stats,
+        [squares(m) for m in (x_full, first_sum, second_sum, attn_out, ffn_out)]
+        + [jnp.sum(valid), 0.0, 0.0]
+    )
+    up_sums = sums(g_pre)
+    norm_sums = [
+        sums(g_attn), gain_one_grad, shift_one_grad, sums(g_ffn), gain_two_grad, shift_two_grad
     ]
-    small = lax.psum(tuple(small), everyone)
-    s_q, s_v, s_up = (own_slice(value, halves, my_half, 0) for value in small[:3])
-    s_o, s_g1, s_s1, s_down, s_g2, s_s2, stats = small[3:]
-    input_rms = jnp.sqrt(stats[:5] / (jnp.maximum(stats[5], 1.0) * width))
-    return (
-        layer_out, input_grad, shard_q, s_q, shard_k, shard_v, s_v, shard_o, s_o,
-        s_g1, s_s1, shard_up, s_up, shard_down, s_down, s_g2, s_s2, input_rms,
+    return finish(
+        layer_out, input_grad, qkv_shard, ffn_shard, up_sums, group_at, norm_sums, stats,
+        sums(dq)[:part], sums(dv)[:part],
     )
 
 

time: 999 us -> 484 us (0.48)
  waiting for transfers between devices: 508 us -> 150 us
  blocking collectives: 143 us -> 0 us
  Pallas kernels: 96.1 us -> 202 us
  matrix products: 102 us -> 0 us
  starting transfers between devices: 7.51 us -> 56.7 us
  local copies, waits for them, and re-layouts: 79.5 us -> 43.1 us
  between operations: 19.8 us -> 3.85 us
  other arithmetic: 33.4 us -> 20.6 us
    all_gather x10 -> x0, waiting for transfers between devices: 193 us -> none  [the longest x6 150 us: local(): lax.all_gather(lax.all_gather(w, 'dp', axis=a, tiled=True), 'tensor', axi...]
    reduce_scatter x7 -> x0, waiting for transfers between devices: 176 us -> none  [the longest x4 116 us: shard(): value = lax.psum_scatter(value, 'dp', scatter_dimension=dp_axis, tiled=True)]
    ppermute x8 -> x59, waiting for transfers between devices: 28.8 us -> 150 us  [the longest x43 102 us: send(): return lax.ppermute(value, ('context', 'tensor'), pairs)]
    pallas_call x2 -> x6, Pallas kernels: 96.1 us -> 202 us  [the longest x1 61.3 us: attend_project(): pl.pallas_call(attend_project_kernel, out_shape=(shape((length // 2, feat...]
    dot_general x12 -> x0, matrix products: 102 us -> none  [the longest x1 18.3 us: local(): g_act = jnp.dot(g_ffn, w_down.T, preferred_element_type=f32)]
    all_gather x7 -> x0, blocking collectives: 101 us -> none  [the longest x4 87.5 us: local(): lax.all_gather(w, 'dp', axis=a, tiled=True)]
    unnamed x28 -> x0, waiting for transfers between devices: 60.4 us -> none
    ppermute x8 -> x59, starting transfers between devices: 6.4 us -> 56.7 us  [the longest x43 33.7 us: send(): return lax.ppermute(value, ('context', 'tensor'), pairs)]
  transfers between devices with their start and end apart: 31 -> 59, of which waited for: 18 -> 20; matrix products, arithmetic and copies ran while one was open for 16% -> 12% of each run, Pallas kernels for 10% -> 33%
where the time goes in v2:
time: 484 us; the launch traced here: 476 us
  Pallas kernels  202 us (42%)
  waiting for transfers between devices  150 us (31%)
  starting transfers between devices  56.7 us (12%)
  local copies, waits for them, and re-layouts  43.1 us (9%)
  other arithmetic  20.6 us (4%)
    ppermute x43, waiting for transfers between devices, send(): return lax.ppermute(value, ('context', 'tensor'), pairs)  102 us
    pallas_call x1, Pallas kernels, attend_project(): pl.pallas_call(attend_project_kernel, out_shape=(shape((length // 2, feat...  61.3 us
    pallas_call x1, Pallas kernels, project_attend(): pl.pallas_call(project_attend_kernel, out_shape=(shape((length // 2, widt...  51.5 us
    pallas_call x1, Pallas kernels, ffn_front(): pl.pallas_call(ffn_front_kernel, out_shape=(shape((rows // 2, width), bf1...  42.1 us
    pallas_call x1, Pallas kernels, ffn_rear(): pl.pallas_call(ffn_rear_kernel, out_shape=(shape((rows, width), f32), sha...  39.8 us
    ppermute x43, starting transfers between devices, send(): return lax.ppermute(value, ('context', 'tensor'), pairs)  33.7 us
    ppermute x12, waiting for transfers between devices, send_deep(): lax.ppermute(value, 'dp', [(i, (i + step) % depth) for i in range(depth)])  33 us
    ppermute x12, starting transfers between devices, send_deep(): lax.ppermute(value, 'dp', [(i, (i + step) % depth) for i in range(depth)])  17.8 us
  transfers between devices with their start and end apart: 59, of which 20 were waited for; matrix products, arithmetic and copies ran while one was open for 12% of the time, Pallas kernels for 33%

profile of v2, /device:TPU:0, one launch (start us, length us, event | category | flops | bytes accessed | tf_op | source)
XLA Modules:
  0.0 476.3 jit_solution(7887446267689956495)
XLA Ops:
  1.6 5.1 %collective-permute-start.3 = (bf16[48,1152]{1,0:T(8,128)(2,1)S(1)}, bf16[48,1152]{1,0:T(8,128)(2,1)S(1)}, u32[]{:S(2)}, u32[]{:S(2)}) collective-permute-start(bf16[48,1152]{1,0:T(8,128)(2,1)S(1)} %fusion.18), channel_id=1, source_target_pairs={{0,24},{8,0},{16,8},{24,16},{1,25},{9,1},{17,9},{25,17},{2,26},{10... | collective-permute-start | bytes 331784 | tf_op jit(solution)/shard_map/ppermute | solution.py:934
  26.9 2.8 collective-permute-start.12
  31.6 6.2 %collective-permute-done.12 = bf16[432,384]{1,0:T(8,128)(2,1)S(1)} collective-permute-done((bf16[432,384]{1,0:T(8,128)(2,1)S(1)}, bf16[432,384]{1,0:T(8,128)(2,1)S(1)}, u32[]{:S(2)}, u32[]{:S(2)}) %collective-permute-start.12) | collective-permute-done | bytes 331808 | tf_op jit(solution)/shard_map/ppermute | solution.py:934
  38.4 21.9 %collective-permute-done.13 = bf16[432,384]{1,0:T(8,128)(2,1)S(1)} collective-permute-done((bf16[432,384]{1,0:T(8,128)(2,1)S(1)}, bf16[432,384]{1,0:T(8,128)(2,1)S(1)}, u32[]{:S(2)}, u32[]{:S(2)}) %collective-permute-start.13) | collective-permute-done | bytes 331808 | tf_op jit(solution)/shard_map/ppermute | solution.py:934
  62.6 19.1 %collective-permute-done.8.n3 = bf16[4,48,1152]{2,1,0:T(8,128)(2,1)S(1)} collective-permute-done((bf16[4,48,1152]{2,1,0:T(8,128)(2,1)}, bf16[4,48,1152]{2,1,0:T(8,128)(2,1)S(1)}, u32[]{:S(2)}, u32[]{:S(2)}) %collective-permute-start.8) | collective-permute-done | bytes 442400 | tf_op jit(solution)/shard_map/ppermute | solution.py:931
  91.8 51.5 %project_attend.1 = (bf16[1024,384]{1,0:T(8,128)(2,1)}, bf16[1024,384]{1,0:T(8,128)(2,1)}, bf16[2048,384]{1,0:T(8,128)(2,1)}, bf16[2048,384]{1,0:T(8,128)(2,1)},...) custom-call(s32[30,11]{1,0:T(8,128)} %pad_add_fusion.table, ...), custom_call_target="tpu_custom_call" | custom-call | flops 52344913920 | bytes 12582912 | tf_op jit(solution)/shard_map/project_attend/pallas_call | solution.py:407
  143.3 17.9 %collective-permute-done.18.g1 = bf16[512,768]{1,0:T(8,128)(2,1)} collective-permute-done((bf16[512,768]{1,0:T(8,128)(2,1)}, bf16[512,768]{1,0:T(8,128)(2,1)}, u32[]{:S(2)}, u32[]{:S(2)}) %collective-permute-start.18) | collective-permute-done | bytes 786464 | tf_op jit(solution)/shard_map/ppermute | solution.py:931
  166.6 4.9 %collective-permute-done.19.att1 = bf16[1024,384]{1,0:T(8,128)(2,1)} collective-permute-done((bf16[1024,384]{1,0:T(8,128)(2,1)}, bf16[1024,384]{1,0:T(8,128)(2,1)}, u32[]{:S(2)}, u32[]{:S(2)}) %collective-permute-start.19) | collective-permute-done | bytes 786464 | tf_op jit(solution)/shard_map/ppermute | solution.py:931
  171.5 42.1 %ffn_front.1 = (bf16[512,768]{1,0:T(8,128)(2,1)}, bf16[512,768]{1,0:T(8,128)(2,1)}, bf16[4,1024,768]{2,1,0:T(8,128)(2,1)}, f32[1024,768]{1,0:T(8,128)}, f32[1024...) custom-call(bf16[1024,384]{1,0:T(8,128)(2,1)} %get-tuple-element.86., ...), custom_call_target="tpu_custom_call" | custom-call | flops 38000001024 | bytes 40000000 | tf_op jit(solution)/shard_map/ffn_front/pallas_call | solution.py:684
  217.1 39.8 %ffn_rear.1 = (f32[1024,768]{1,0:T(8,128)}, bf16[1024,384]{1,0:T(8,128)(2,1)}, bf16[1024,384]{1,0:T(8,128)(2,1)}, bf16[4,4,240,384]{3,2,1,0:T(8,128)(2,1)}, bf16...) custom-call(bf16[1024,384]{1,0:T(8,128)(2,1)} %get-tuple-element.86.att0, ...), custom_call_target="tpu_custom_call" | custom-call | flops 38000001024 | bytes 40000000 | tf_op jit(solution)/shard_map/ffn_rear/pallas_call | solution.py:820
  263.2 3.1 add_convert_fusion.1
  275.9 8.2 %collective-permute-done.30 = bf16[4,192,384]{2,1,0:T(8,128)(2,1)S(1)} collective-permute-done((bf16[4,192,384]{2,1,0:T(8,128)(2,1)S(1)}, bf16[4,192,384]{2,1,0:T(8,128)(2,1)S(1)}, u32[]{:S(2)}, u32[]{:S(2)}) %collective-permute-start.30) | collective-permute-done | bytes 589856 | tf_op jit(solution)/shard_map/ppermute | solution.py:931
  286.5 61.3 %attend_project.1 = (f32[1024,768]{1,0:T(8,128)}, bf16[1024,768]{1,0:T(8,128)(2,1)}, bf16[2,4,48,1152]{3,2,1,0:T(8,128)(2,1)}, bf16[2,4,48,1152]{3,2,1,0:T(8,128)(2,1)}, f32[8,384]{1,0:T(8,128)}) custom-call(s32[30,11]{1,0:T(8,128)} %pad_add_fusion.table, s32[2]{0:T(128)} %fusion.42.wide, bf16[512,768]{1,0:T(8,128)(2,1)} %copy-done.10, ...), custom_call_target="tpu_custom_call" | custom-call | flops 68451041280 | bytes 23592960 | tf_op jit(solution)/shard_map/attend_project/pallas_call | solution.py:492
  354.8 3.8 collective-permute-start.56
  366.1 3.5 collective-permute-done.51
  370.2 9.5 %collective-permute-done.52 = f32[9224]{0:T(1024)S(1)} collective-permute-done((f32[9224]{0:T(1024)S(1)}, f32[9224]{0:T(1024)S(1)}, u32[]{:S(2)}, u32[]{:S(2)}) %collective-permute-start.52) | collective-permute-done | bytes 36928 | tf_op jit(solution)/shard_map/ppermute | solution.py:990
  379.7 4.1 collective-permute-start.53
  383.7 2.9 gather_chunks.2
  401.3 3.6 collective-permute-done.42
  404.9 7.4 %collective-permute-done.43 = bf16[4,48,1152]{2,1,0:T(8,128)(2,1)S(1)} collective-permute-done((bf16[4,48,1152]{2,1,0:T(8,128)(2,1)S(1)}, bf16[4,48,1152]{2,1,0:T(8,128)(2,1)S(1)}, u32[]{:S(2)}, u32[]{:S(2)}) %collective-permute-start.43) | collective-permute-done | bytes 442400 | tf_op jit(solution)/shard_map/ppermute | solution.py:931
  412.3 4.3 collective-permute-done.41
  427.5 3.5 collective-permute-done.47
  442.0 27.8 %collective-permute-done.37.c1 = bf16[512,768]{1,0:T(8,128)(2,1)S(1)} collective-permute-done((bf16[512,768]{1,0:T(8,128)(2,1)}, bf16[512,768]{1,0:T(8,128)(2,1)S(1)}, u32[]{:S(2)}, u32[]{:S(2)}) %collective-permute-start.37) | collective-permute-done | bytes 786464 | tf_op jit(solution)/shard_map/ppermute | solution.py:931
  471.9 4.1 gather_chunks.3
  (324 shorter events, 114.2 us)
Async XLA Ops:
  13.3 68.6 %collective-permute-start = (bf16[512,768]{1,0:T(8,128)(2,1)S(1)}, bf16[512,768]{1,0:T(8,128)(2,1)}, u32[]{:S(2)}, u32[]{:S(2)}) collective-permute-start(bf16[512,768]{1,0:T(8,128)(2,1)S(1)} %get-tuple-element.166), channel_id=1, source_target_pairs={{0,4},{2,6},{4,0},{6,2},{1,5},{3,7},{5,1},{7,3},{8,12},{10,14},{12... | collective-permute-start | bytes 2359304 | tf_op jit(solution)/shard_map/ppermute | solution.py:931
  25.7 60.3 %collective-permute-start.1 = (bf16[512,768]{1,0:T(8,128)(2,1)S(1)}, bf16[512,768]{1,0:T(8,128)(2,1)}, u32[]{:S(2)}, u32[]{:S(2)}) collective-permute-start(bf16[512,768]{1,0:T(8,128)(2,1)S(1)} %get-tuple-element.167.x0), channel_id=1, source_target_pairs={{0,2},{2,0},{4,6},{6,4},{1,3},{3,1},{5,7},{7,5},{8,10},{10,8},{12,... | collective-permute-start | bytes 2359304 | tf_op jit(solution)/shard_map/ppermute | solution.py:931
  29.9 30.4 %collective-permute-start.13 = (bf16[432,384]{1,0:T(8,128)(2,1)S(1)}, bf16[432,384]{1,0:T(8,128)(2,1)S(1)}, u32[]{:S(2)}, u32[]{:S(2)}) collective-permute-start(bf16[432,384]{1,0:T(8,128)(2,1)S(1)} %pad_maximum_fusion.6), channel_id=1, source_target_pairs={{0,16},{8,24},{16,0},{24,8},{1,17},{9,25},{17,1},{25,9},{2,18},{10... | collective-permute-start | bytes 995336 | tf_op jit(solution)/shard_map/ppermute | solution.py:934
  84.5 76.7 %collective-permute-start.15 = (bf16[4,432,384]{2,1,0:T(8,128)(2,1)}, bf16[4,432,384]{2,1,0:T(8,128)(2,1)}, u32[]{:S(2)}, u32[]{:S(2)}) collective-permute-start(bf16[4,432,384]{2,1,0:T(8,128)(2,1)} %constant_dynamic-slice_fusion.2.rest_0_), channel_id=1, source_target_pairs={{0,4},{2,6},{4,0},{6,2},{1,5},{3,7},{5,1},{7,3},{8,12},{10,14},{12... | collective-permute-start | bytes 3981320 | tf_op jit(solution)/shard_map/ppermute | solution.py:931
  86.0 75.2 %collective-permute-start.16 = (bf16[4,432,384]{2,1,0:T(8,128)(2,1)}, bf16[4,432,384]{2,1,0:T(8,128)(2,1)}, u32[]{:S(2)}, u32[]{:S(2)}) collective-permute-start(bf16[4,432,384]{2,1,0:T(8,128)(2,1)} %constant_dynamic-slice_fusion.2.rest_0_), channel_id=1, source_target_pairs={{0,1},{2,3},{4,5},{6,7},{1,0},{3,2},{5,4},{7,6},{8,9},{10,11},{12,... | collective-permute-start | bytes 3981320 | tf_op jit(solution)/shard_map/ppermute | solution.py:931
  86.5 74.7 %collective-permute-start.17 = (bf16[4,432,384]{2,1,0:T(8,128)(2,1)}, bf16[4,432,384]{2,1,0:T(8,128)(2,1)}, u32[]{:S(2)}, u32[]{:S(2)}) collective-permute-start(bf16[4,432,384]{2,1,0:T(8,128)(2,1)} %constant_dynamic-slice_fusion.2.rest_0_), channel_id=1, source_target_pairs={{0,5},{2,7},{4,1},{6,3},{1,4},{3,6},{5,0},{7,2},{8,13},{10,15},{12... | collective-permute-start | bytes 3981320 | tf_op jit(solution)/shard_map/ppermute | solution.py:931
  88.0 73.2 %collective-permute-start.18 = (bf16[512,768]{1,0:T(8,128)(2,1)}, bf16[512,768]{1,0:T(8,128)(2,1)}, u32[]{:S(2)}, u32[]{:S(2)}) collective-permute-start(bf16[512,768]{1,0:T(8,128)(2,1)} %get-tuple-element.85), channel_id=1, source_target_pairs={{0,4},{2,6},{4,0},{6,2},{1,5},{3,7},{5,1},{7,3},{8,12},{10,14},{12... | collective-permute-start | bytes 2359304 | tf_op jit(solution)/shard_map/ppermute | solution.py:931
  213.6 43.3 %collective-permute-start.24 = (bf16[512,768]{1,0:T(8,128)(2,1)}, bf16[512,768]{1,0:T(8,128)(2,1)}, u32[]{:S(2)}, u32[]{:S(2)}) collective-permute-start(bf16[512,768]{1,0:T(8,128)(2,1)} %get-tuple-element.95), channel_id=1, source_target_pairs={{0,4},{2,6},{4,0},{6,2},{1,5},{3,7},{5,1},{7,3},{8,12},{10,14},{12... | collective-permute-start | bytes 2359304 | tf_op jit(solution)/shard_map/ppermute | solution.py:931
  215.2 41.8 %collective-permute-start.26 = (bf16[512,768]{1,0:T(8,128)(2,1)}, bf16[512,768]{1,0:T(8,128)(2,1)}, u32[]{:S(2)}, u32[]{:S(2)}) collective-permute-start(bf16[512,768]{1,0:T(8,128)(2,1)} %get-tuple-element.95), channel_id=1, source_target_pairs={{0,5},{2,7},{4,1},{6,3},{1,4},{3,6},{5,0},{7,2},{8,13},{10,15},{12... | collective-permute-start | bytes 2359304 | tf_op jit(solution)/shard_map/ppermute | solution.py:931
  215.6 41.3 %collective-permute-start.27 = (bf16[4,4,192,384]{3,2,1,0:T(8,128)(2,1)}, bf16[4,4,192,384]{3,2,1,0:T(8,128)(2,1)}, u32[]{:S(2)}, u32[]{:S(2)}) collective-permute-start(bf16[4,4,192,384]{3,2,1,0:T(8,128)(2,1)} %get-tuple-element.96), channel_id=1, source_target_pairs={{0,2},{2,0},{4,6},{6,4},{1,3},{3,1},{5,7},{7,5},{8,10},{10,8},{12,... | collective-permute-start | bytes 7077896 | tf_op jit(solution)/shard_map/ppermute | solution.py:931
  215.7 41.3 %collective-permute-start.25 = (bf16[512,768]{1,0:T(8,128)(2,1)}, bf16[512,768]{1,0:T(8,128)(2,1)}, u32[]{:S(2)}, u32[]{:S(2)}) collective-permute-start(bf16[512,768]{1,0:T(8,128)(2,1)} %get-tuple-element.107.c0), channel_id=1, source_target_pairs={{0,1},{2,3},{4,5},{6,7},{1,0},{3,2},{5,4},{7,6},{8,9},{10,11},{12,... | collective-permute-start | bytes 2359304 | tf_op jit(solution)/shard_map/ppermute | solution.py:931
  269.2 78.7 %collective-permute-start.31 = (bf16[4,192,384]{2,1,0:T(8,128)(2,1)}, bf16[4,192,384]{2,1,0:T(8,128)(2,1)}, u32[]{:S(2)}, u32[]{:S(2)}) collective-permute-start(bf16[4,192,384]{2,1,0:T(8,128)(2,1)} %get-tuple-element.173), channel_id=1, source_target_pairs={{0,1},{2,3},{4,5},{6,7},{1,0},{3,2},{5,4},{7,6},{8,9},{10,11},{12,... | collective-permute-start | bytes 1769480 | tf_op jit(solution)/shard_map/ppermute | solution.py:931
  269.7 78.1 %collective-permute-start.32 = (bf16[4,192,384]{2,1,0:T(8,128)(2,1)}, bf16[4,192,384]{2,1,0:T(8,128)(2,1)}, u32[]{:S(2)}, u32[]{:S(2)}) collective-permute-start(bf16[4,192,384]{2,1,0:T(8,128)(2,1)} %get-tuple-element.172), channel_id=1, source_target_pairs={{0,5},{2,7},{4,1},{6,3},{1,4},{3,6},{5,0},{7,2},{8,13},{10,15},{12... | collective-permute-start | bytes 1769480 | tf_op jit(solution)/shard_map/ppermute | solution.py:931
  273.8 74.1 %collective-permute-start.33 = (bf16[4,240,384]{2,1,0:T(8,128)(2,1)}, bf16[4,240,384]{2,1,0:T(8,128)(2,1)}, u32[]{:S(2)}, u32[]{:S(2)}) collective-permute-start(bf16[4,240,384]{2,1,0:T(8,128)(2,1)} %get-tuple-element.170), channel_id=1, source_target_pairs={{0,4},{2,6},{4,0},{6,2},{1,5},{3,7},{5,1},{7,3},{8,12},{10,14},{12... | collective-permute-start | bytes 2211848 | tf_op jit(solution)/shard_map/ppermute | solution.py:931
  275.3 72.6 %collective-permute-start.34 = (bf16[4,240,384]{2,1,0:T(8,128)(2,1)}, bf16[4,240,384]{2,1,0:T(8,128)(2,1)}, u32[]{:S(2)}, u32[]{:S(2)}) collective-permute-start(bf16[4,240,384]{2,1,0:T(8,128)(2,1)} %get-tuple-element.169), channel_id=1, source_target_pairs={{0,1},{2,3},{4,5},{6,7},{1,0},{3,2},{5,4},{7,6},{8,9},{10,11},{12,... | collective-permute-start | bytes 2211848 | tf_op jit(solution)/shard_map/ppermute | solution.py:931
  285.0 62.9 %collective-permute-start.35 = (bf16[4,240,384]{2,1,0:T(8,128)(2,1)}, bf16[4,240,384]{2,1,0:T(8,128)(2,1)}, u32[]{:S(2)}, u32[]{:S(2)}) collective-permute-start(bf16[4,240,384]{2,1,0:T(8,128)(2,1)} %get-tuple-element.168), channel_id=1, source_target_pairs={{0,5},{2,7},{4,1},{6,3},{1,4},{3,6},{5,0},{7,2},{8,13},{10,15},{12... | collective-permute-start | bytes 2211848 | tf_op jit(solution)/shard_map/ppermute | solution.py:931
  350.1 40.1 %collective-permute-start.40 = (bf16[2,4,48,1152]{3,2,1,0:T(8,128)(2,1)}, bf16[2,4,48,1152]{3,2,1,0:T(8,128)(2,1)}, u32[]{:S(2)}, u32[]{:S(2)}) collective-permute-start(bf16[2,4,48,1152]{3,2,1,0:T(8,128)(2,1)} %get-tuple-element.131), channel_id=1, source_target_pairs={{0,2},{2,0},{4,6},{6,4},{1,3},{3,1},{5,7},{7,5},{8,10},{10,8},{12,... | collective-permute-start | bytes 2654216 | tf_op jit(solution)/shard_map/ppermute | solution.py:931
  354.8 33.4 %collective-permute-start.54 = (bf16[432,384]{1,0:T(8,128)(2,1)}, bf16[432,384]{1,0:T(8,128)(2,1)}, u32[]{:S(2)}, u32[]{:S(2)}) collective-permute-start(bf16[432,384]{1,0:T(8,128)(2,1)} %get-tuple-element.186), channel_id=1, source_target_pairs={{0,8},{8,16},{16,24},{24,0},{1,9},{9,17},{17,25},{25,1},{2,10},{10... | collective-permute-start | bytes 995336 | tf_op jit(solution)/shard_map/ppermute | solution.py:934
  354.8 33.4 %collective-permute-start.55 = (bf16[432,384]{1,0:T(8,128)(2,1)S(1)}, bf16[432,384]{1,0:T(8,128)(2,1)}, u32[]{:S(2)}, u32[]{:S(2)}) collective-permute-start(bf16[432,384]{1,0:T(8,128)(2,1)S(1)} %get-tuple-element.188), channel_id=1, source_target_pairs={{0,16},{8,24},{16,0},{24,8},{1,17},{9,25},{17,1},{25,9},{2,18},{10... | collective-permute-start | bytes 995336 | tf_op jit(solution)/shard_map/ppermute | solution.py:934
  354.8 33.4 %collective-permute-start.56 = (bf16[432,384]{1,0:T(8,128)(2,1)S(1)}, bf16[432,384]{1,0:T(8,128)(2,1)}, u32[]{:S(2)}, u32[]{:S(2)}) collective-permute-start(bf16[432,384]{1,0:T(8,128)(2,1)S(1)} %get-tuple-element.187), channel_id=1, source_target_pairs={{0,24},{8,0},{16,8},{24,16},{1,25},{9,1},{17,9},{25,17},{2,26},{10... | collective-permute-start | bytes 995336 | tf_op jit(solution)/shard_map/ppermute | solution.py:934
  399.8 31.4 %collective-permute-start.36 = (bf16[1024,768]{1,0:T(8,128)(2,1)S(1)}, bf16[1024,768]{1,0:T(8,128)(2,1)S(1)}, u32[]{:S(2)}, u32[]{:S(2)}) collective-permute-start(bf16[1024,768]{1,0:T(8,128)(2,1)S(1)} %copy-done.28), channel_id=1, source_target_pairs={{0,2},{2,0},{4,6},{6,4},{1,3},{3,1},{5,7},{7,5},{8,10},{10,8},{12,... | collective-permute-start | bytes 4718600 | tf_op jit(solution)/shard_map/ppermute | solution.py:931
  432.8 37.0 %collective-permute-start.37 = (bf16[512,768]{1,0:T(8,128)(2,1)}, bf16[512,768]{1,0:T(8,128)(2,1)S(1)}, u32[]{:S(2)}, u32[]{:S(2)}) collective-permute-start(bf16[512,768]{1,0:T(8,128)(2,1)} %get-tuple-element.178), channel_id=1, source_target_pairs={{0,4},{2,6},{4,0},{6,2},{1,5},{3,7},{5,1},{7,3},{8,12},{10,14},{12... | collective-permute-start | bytes 2359304 | tf_op jit(solution)/shard_map/ppermute | solution.py:931
  433.3 38.6 %collective-permute-start.39 = (bf16[512,768]{1,0:T(8,128)(2,1)}, bf16[512,768]{1,0:T(8,128)(2,1)}, u32[]{:S(2)}, u32[]{:S(2)}) collective-permute-start(bf16[512,768]{1,0:T(8,128)(2,1)} %get-tuple-element.178), channel_id=1, source_target_pairs={{0,5},{2,7},{4,1},{6,3},{1,4},{3,6},{5,0},{7,2},{8,13},{10,15},{12... | collective-permute-start | bytes 2359304 | tf_op jit(solution)/shard_map/ppermute | solution.py:931
  435.7 35.3 %collective-permute-start.38 = (bf16[512,768]{1,0:T(8,128)(2,1)S(1)}, bf16[512,768]{1,0:T(8,128)(2,1)S(1)}, u32[]{:S(2)}, u32[]{:S(2)}) collective-permute-start(bf16[512,768]{1,0:T(8,128)(2,1)S(1)} %get-tuple-element.179.c0), channel_id=1, source_target_pairs={{0,1},{2,3},{4,5},{6,7},{1,0},{3,2},{5,4},{7,6},{8,9},{10,11},{12,... | collective-permute-start | bytes 2359304 | tf_op jit(solution)/shard_map/ppermute | solution.py:931
  (68 other events, 1017.5 us)
